TPU v7x, 32 devices: a whole 2x2x4 slice. The times are simulated.
32 devices in a mesh: groups: 2 (over x), expert: 4 (over y, core), donor: 4 (over z).
Axes of the slice: x: 2, y: 2, z: 4, core: 2. Of those that a mesh axis runs over, the one named last changes fastest.
Arguments:
- hidden_in: bfloat16 [1024, 4096], P(('groups', 'expert')), parts along dimension 0, may hold values from -6 to 6
- queries: bfloat16 [1024, 4096], P(('groups', 'expert'), 'donor'), parts along dimension 0, may hold values from -39 to 39
- suffix_kv: bfloat16 [1024, 2, 256], P(('groups', 'expert')), parts along dimension 0, may hold values from -12 to 12
- kv_pool: bfloat16 [128, 2, 32, 256], P(('groups', 'expert', 'donor')), parts along dimension 0, may hold values from -12 to 12
- page_table: int32 [8, 16], P('groups'), parts along dimension 0, may hold values from 0 to 63, as said below
- prefix_len: int32 [8], P('groups'), parts along dimension 0, may hold values from 1 to 512, as said below
- out_weight: bfloat16 [4096, 4096], P('donor', 'expert'), may hold values from -0.09375 to 0.09375
- norm_gain: bfloat16 [4096], replicated, may hold values from 0.099609375 to 1.8984375
- expert_ids: int32 [1024, 4], P(('groups', 'expert')), parts along dimension 0, may hold values from 0 to 7, all different within a row; in each aligned block of 128 rows (0 to 127, 128 to 255, ...) at most 80 rows name the same one
- route_probs: float32 [1024, 4], P(('groups', 'expert')), parts along dimension 0, may hold values from 0.05 to 1
- w_gate_up: bfloat16 [16, 4096, 2, 768], P(('expert', 'donor')), may hold values from -0.09375 to 0.09375
- w_down: bfloat16 [16, 768, 4096], P(('expert', 'donor')), may hold values from -0.15625 to 0.15625
Outputs:
- layer_out: bfloat16 [1024, 4096], P(('groups', 'expert'), 'donor'), parts along dimension 0
- head_out: bfloat16 [1024, 4096], P(('groups', 'expert'), 'donor'), parts along dimension 0
There are 2 independent parts, one for each index of `groups`. A program takes and returns all parts, laid end to end along the dimension named above; an argument that names none is the same for every part. Nothing has to cross between parts.
Inputs may be any that keep to these rules, and one draw needn't show every extreme that they name: For every sequence s the values page_table[s, j] // 4 over j are 0 to 15, each once; pages b * 4 to b * 4 + 3 hold one page of every sequence. `prefix_len`: in every draw one sequence has the longest prefix, 512 tokens. `expert_ids`: the 4 experts of a token differ. Among the 128 tokens of one sequence no expert is named by more than 80 tokens, and in some sequence of every draw some expert is named by exactly 80.
All inputs are finite; a program needn't handle non-finite values.
Results may differ from a plain program's by a relative error of at most 0.0056.
Values may be sent and summed in bfloat16 or wider, within the bound.
A program may use at most 128 MiB of HBM per device.

v0:
```python
import functools

import jax
import jax.numpy as jnp
from jax import lax
from jax.experimental import pallas as pl
from jax.experimental.pallas import tpu as pltpu
from jax.sharding import PartitionSpec as P

MESH = pl.DeviceIdType.MESH


def place():
    expert = lax.axis_index("expert")
    return expert // 2, lax.rem(expert, 2), lax.axis_index("donor")


def send(src, dst, sends, recvs, slot, **where):
    return pltpu.make_async_remote_copy(
        src_ref=src,
        dst_ref=dst,
        send_sem=sends.at[slot],
        recv_sem=recvs.at[slot],
        device_id=where,
        device_id_type=MESH,
    )


def greet(chips, donors):
    row, core, donor = place()
    barrier = pltpu.get_barrier_semaphore()
    pl.semaphore_signal(
        barrier, inc=1, device_id={"expert": row * 2 + 1 - core}, device_id_type=MESH
    )
    for step in range(1, chips):
        other = lax.rem(row + step, chips) * 2 + core
        pl.semaphore_signal(barrier, inc=1, device_id={"expert": other}, device_id_type=MESH)
    for step in range(1, donors):
        other = lax.rem(donor + step, donors)
        pl.semaphore_signal(barrier, inc=1, device_id={"donor": other}, device_id_type=MESH)
    pl.semaphore_wait(barrier, chips + donors - 1)


def far_first(donors):
    return sorted(range(1, donors), key=lambda k: (-min(k, donors - k), k))


def gather_kernel(
    chips,
    donors,
    heads_ref,
    out_ref,
    hidden_ref,
    full_ref,
    terms_ref,
    terms_in,
    block_ref,
    own_sem,
    t_send,
    t_recv,
    z_send,
    z_recv,
    y_send,
    y_recv,
    c_send,
    c_recv,
):
    row, core, donor = place()
    rows, cols = block_ref.shape
    greet(chips, donors)
    strip = 16

    def project(step_z, slot):
        top = pl.multiple_of(lax.rem(donor + step_z, donors) * rows, rows)
        terms_ref[slot] = jnp.dot(
            heads_ref[pl.ds(top, rows), :], out_ref[...], preferred_element_type=jnp.float32
        ).astype(terms_ref.dtype)

    term_copies = {}
    for step in far_first(donors):
        project(step, step)
        copy = send(
            terms_ref.at[step],
            terms_in.at[step - 1],
            t_send,
            t_recv,
            step - 1,
            donor=lax.rem(donor + step, donors),
        )
        copy.start()
        term_copies[step] = copy
    project(0, 0)
    for step in far_first(donors):
        term_copies[step].wait_recv()

    def add(index, carry):
        at = pl.ds(pl.multiple_of(index * strip, strip), strip)
        value = terms_ref[0, at, :].astype(jnp.float32)
        for step in range(1, donors):
            value = value + terms_in[step - 1, at, :].astype(jnp.float32)
        value = value + hidden_ref[at, :].astype(jnp.float32)
        block_ref[at, :] = value.astype(block_ref.dtype)
        return carry

    lax.fori_loop(0, rows // strip, add, 0)

    def slot_of(donor_from, row_from, core_from):
        top = pl.multiple_of(donor_from * rows, rows)
        left = pl.multiple_of((row_from * 2 + core_from) * cols, cols)
        return full_ref.at[pl.ds(top, rows), pl.ds(left, cols)]

    own = pltpu.make_async_copy(block_ref, slot_of(donor, row, core), own_sem)
    own.start()
    started = []

    def along_y(src, step_z, donor_from):
        for step in range(1, chips):
            copy = send(
                src,
                slot_of(donor_from, row, core),
                y_send,
                y_recv,
                step_z * (chips - 1) + step - 1,
                expert=lax.rem(row + step, chips) * 2 + core,
            )
            copy.start()
            started.append(copy)

    def beside(src, step_z, step_y, donor_from, row_from):
        copy = send(
            src,
            slot_of(donor_from, row_from, core),
            c_send,
            c_recv,
            step_z * chips + step_y,
            expert=row * 2 + 1 - core,
        )
        copy.start()
        started.append(copy)

    along_y(block_ref, 0, donor)
    z_copies = {}
    near_first = far_first(donors)[::-1]
    for step in near_first:
        copy = send(
            block_ref,
            slot_of(donor, row, core),
            z_send,
            z_recv,
            step - 1,
            donor=lax.rem(donor + step, donors),
        )
        copy.start()
        z_copies[step] = copy
    beside(block_ref, 0, 0, donor, row)

    def take_y(step_z, donor_from):
        for step in range(1, chips):
            row_from = lax.rem(row + chips - step, chips)
            there = slot_of(donor_from, row_from, core)
            send(
                there,
                there,
                y_send,
                y_recv,
                step_z * (chips - 1) + step - 1,
                expert=row_from * 2 + core,
            ).wait_recv()
            beside(there, step_z, step, donor_from, row_from)

    for step in near_first:
        donor_from = lax.rem(donor + donors - step, donors)
        there = slot_of(donor_from, row, core)
        send(there, there, z_send, z_recv, step - 1, donor=donor_from).wait_recv()
        along_y(there, step, donor_from)
        beside(there, step, 0, donor_from, row)
    for step in [0] + near_first:
        take_y(step, lax.rem(donor + donors - step, donors))
    for step_z in range(donors):
        donor_from = lax.rem(donor + donors - step_z, donors)
        for step_y in range(chips):
            row_from = lax.rem(row + chips - step_y, chips)
            there = slot_of(donor_from, row_from, 1 - core)
            send(
                there, there, c_send, c_recv, step_z * chips + step_y, expert=row * 2 + 1 - core
            ).wait_recv()
    own.wait()
    for copy in list(term_copies.values()) + list(z_copies.values()) + started:
        copy.wait_send()


def gather_blocks(heads, out_weight, block, chips, donors):
    rows, cols = block.shape
    dma = pltpu.SemaphoreType.DMA
    return pl.pallas_call(
        functools.partial(gather_kernel, chips, donors),
        out_shape=jax.ShapeDtypeStruct((rows * donors, cols * chips * 2), block.dtype),
        in_specs=[pl.BlockSpec(memory_space=pltpu.VMEM)] * 3,
        out_specs=pl.BlockSpec(memory_space=pltpu.VMEM),
        scratch_shapes=[
            pltpu.VMEM((donors, rows, cols), block.dtype),
            pltpu.VMEM((donors - 1, rows, cols), block.dtype),
            pltpu.VMEM((rows, cols), block.dtype),
            dma,
            dma((donors - 1,)),
            dma((donors - 1,)),
            dma((donors - 1,)),
            dma((donors - 1,)),
            dma((donors * (chips - 1),)),
            dma((donors * (chips - 1),)),
            dma((donors * chips,)),
            dma((donors * chips,)),
        ],
        compiler_params=pltpu.CompilerParams(collective_id=1, has_side_effects=True),
        name="gather_blocks",
    )(heads, out_weight, block)


def reduce_kernel(
    chips,
    donors,
    act_ref,
    down_ref,
    total_ref,
    part_ref,
    c_in,
    y_out,
    y_in,
    z_out,
    z_in,
    c_send,
    c_recv,
    y_send,
    y_recv,
    z_send,
    z_recv,
):
    row, core, donor = place()
    rows, cols = total_ref.shape
    greet(chips, donors)
    order = far_first(donors) + [0]
    strip = 16

    def tile(row_to, core_to, step_z):
        top = pl.multiple_of((row_to * 2 + core_to) * rows, rows)
        left = pl.multiple_of(lax.rem(donor + step_z, donors) * cols, cols)
        return part_ref.at[pl.ds(top, rows), pl.ds(left, cols)]

    def add(out, *terms):
        def body(index, carry):
            at = pl.ds(pl.multiple_of(index * strip, strip), strip)
            value = terms[0][at, :].astype(jnp.float32)
            for term in terms[1:]:
                value = value + term[at, :].astype(jnp.float32)
            out[at, :] = value.astype(out.dtype)
            return carry

        lax.fori_loop(0, rows // strip, body, 0)

    started = []
    arrivals = {}

    def multiply(step_z):
        left = pl.multiple_of(lax.rem(donor + step_z, donors) * cols, cols)

        def body(index, carry):
            at = pl.ds(pl.multiple_of(index * rows, rows), rows)
            part_ref[at, pl.ds(left, cols)] = jnp.dot(
                act_ref[at, :],
                down_ref[:, pl.ds(left, cols)],
                preferred_element_type=jnp.float32,
            ).astype(part_ref.dtype)
            return carry

        lax.fori_loop(0, chips * 2, body, 0)

    def beside(step_z):
        for step_y in range(chips - 1, -1, -1):
            slot = step_z * chips + step_y
            copy = send(
                tile(lax.rem(row + step_y, chips), 1 - core, step_z),
                c_in.at[slot],
                c_send,
                c_recv,
                slot,
                expert=row * 2 + 1 - core,
            )
            copy.start()
            started.append(copy)

    def along_y(step_z):
        for step_y in range(chips - 1, 0, -1):
            row_to = lax.rem(row + step_y, chips)
            slot = step_z * chips + step_y
            send(
                c_in.at[slot], c_in.at[slot], c_send, c_recv, slot, expert=row * 2 + 1 - core
            ).wait_recv()
            hop = step_z * (chips - 1) + step_y - 1
            add(y_out.at[hop], tile(row_to, core, step_z), c_in.at[slot])
            copy = send(
                y_out.at[hop], y_in.at[hop], y_send, y_recv, hop, expert=row_to * 2 + core
            )
            copy.start()
            arrivals[hop] = copy
            started.append(copy)

    for index, step_z in enumerate(order):
        multiply(step_z)
        beside(step_z)
        if index:
            along_y(order[index - 1])
    along_y(order[-1])
    for step_z in order:
        slot = step_z * chips
        send(
            c_in.at[slot], c_in.at[slot], c_send, c_recv, slot, expert=row * 2 + 1 - core
        ).wait_recv()
        terms = [tile(row, core, step_z), c_in.at[slot]]
        for step_y in range(1, chips):
            hop = step_z * (chips - 1) + step_y - 1
            arrivals[hop].wait_recv()
            terms.append(y_in.at[hop])
        if step_z:
            add(z_out.at[step_z - 1], *terms)
            copy = send(
                z_out.at[step_z - 1],
                z_in.at[step_z - 1],
                z_send,
                z_recv,
                step_z - 1,
                donor=lax.rem(donor + step_z, donors),
            )
            copy.start()
            arrivals["z", step_z] = copy
            started.append(copy)
        else:
            for step in order[:-1]:
                arrivals["z", step].wait_recv()
                terms.append(z_in.at[step - 1])
            add(total_ref, *terms)
    for copy in started:
        copy.wait_send()


def reduce_blocks(activated, down, chips, donors):
    rows, cols = activated.shape[0] // (chips * 2), down.shape[1] // donors
    dma = pltpu.SemaphoreType.DMA
    held = lambda count: pltpu.VMEM((count, rows, cols), activated.dtype)
    return pl.pallas_call(
        functools.partial(reduce_kernel, chips, donors),
        out_shape=jax.ShapeDtypeStruct((rows, cols), jnp.float32),
        in_specs=[pl.BlockSpec(memory_space=pltpu.VMEM)] * 2,
        out_specs=pl.BlockSpec(memory_space=pltpu.VMEM),
        scratch_shapes=[
            pltpu.VMEM((activated.shape[0], down.shape[1]), activated.dtype),
            held(donors * chips),
            held(donors * (chips - 1)),
            held(donors * (chips - 1)),
            held(donors - 1),
            held(donors - 1),
            dma((donors * chips,)),
            dma((donors * chips,)),
            dma((donors * (chips - 1),)),
            dma((donors * (chips - 1),)),
            dma((donors - 1,)),
            dma((donors - 1,)),
        ],
        compiler_params=pltpu.CompilerParams(collective_id=2, has_side_effects=True),
        name="reduce_blocks",
    )(activated, down)


def shards(
    hidden_in,
    queries,
    suffix_kv,
    kv_pool,
    page_table,
    prefix_len,
    out_weight,
    norm_gain,
    expert_ids,
    route_probs,
    w_gate_up,
    w_down,
):
    n_expert = lax.axis_size("expert")
    n_donor = lax.axis_size("donor")
    expert_index = lax.axis_index("expert")
    donor_index = lax.axis_index("donor")
    share_count = n_donor // 2
    seq_count, page_count = page_table.shape
    suffix_len = queries.shape[0]
    kv_heads = suffix_kv.shape[1]
    head_dim = suffix_kv.shape[2] // 2
    page_len = kv_pool.shape[2]
    model_width = hidden_in.shape[1]
    columns = model_width // n_donor
    experts_all = 2 * n_expert
    ff_local = w_gate_up.shape[3]
    my_group = donor_index * kv_heads // n_donor
    owner_index = expert_index * n_donor + donor_index
    owner_of = page_table // seq_count
    held_slot = jnp.sum(jnp.where(owner_of == owner_index, page_table % seq_count, 0), axis=1)
    dest_group = jnp.arange(n_donor, dtype=jnp.int32) * kv_heads // n_donor
    wanted = (held_slot[:, None] * kv_heads + dest_group[None, :]).reshape(-1)
    outgoing = jnp.take(
        kv_pool.reshape(seq_count * kv_heads, page_len, 2 * head_dim), wanted, axis=0
    )
    arrived = lax.all_to_all(outgoing, ("expert", "donor"), split_axis=0, concat_axis=0, tiled=True)
    my_owners = lax.dynamic_index_in_dim(owner_of, expert_index, 0, keepdims=False)
    ordered = jnp.take(arrived, my_owners, axis=0).reshape(page_count * page_len, 2 * head_dim)
    prefix_keys = ordered[:, :head_dim]
    prefix_vals = ordered[:, head_dim:]
    score_scale = head_dim ** (-0.5)
    query_heads = queries.reshape(suffix_len, -1, head_dim)
    fresh_pair = lax.dynamic_index_in_dim(suffix_kv, my_group, 1, keepdims=False)
    causal = jnp.arange(suffix_len)[:, None] >= jnp.arange(suffix_len)[None, :]
    fresh_scores = (
        jnp.einsum(
            "thc,uc->thu", query_heads, fresh_pair[:, :head_dim], preferred_element_type=jnp.float32
        )
        * score_scale
    )
    fresh_scores = jnp.where(causal[:, None, :], fresh_scores, -jnp.inf)
    prefix_tokens = lax.dynamic_index_in_dim(prefix_len, expert_index, 0, keepdims=False)
    block_keys = min(1024, page_count * page_len)
    live_blocks = (prefix_tokens + block_keys - 1) // block_keys

    def block_scores(block_index):
        keys_block = lax.dynamic_slice_in_dim(prefix_keys, block_index * block_keys, block_keys, 0)
        raw_scores = (
            jnp.einsum("thc,kc->thk", query_heads, keys_block, preferred_element_type=jnp.float32)
            * score_scale
        )
        visible = block_index * block_keys + jnp.arange(block_keys) < prefix_tokens
        return jnp.where(visible[None, None, :], raw_scores, -jnp.inf)

    def raise_max(block_index, running):
        return jnp.maximum(running, jnp.max(block_scores(block_index), axis=2))

    row_max = lax.fori_loop(0, live_blocks, raise_max, jnp.max(fresh_scores, axis=2))

    def add_block(block_index, loop_state):
        row_total, weighted = loop_state
        exp_scores = jnp.exp(block_scores(block_index) - row_max[:, :, None])
        vals_block = lax.dynamic_slice_in_dim(prefix_vals, block_index * block_keys, block_keys, 0)
        weighted = weighted + jnp.einsum(
            "thk,kc->thc",
            exp_scores.astype(jnp.bfloat16),
            vals_block,
            preferred_element_type=jnp.float32,
        )
        return (row_total + jnp.sum(exp_scores, axis=2), weighted)

    fresh_exp = jnp.exp(fresh_scores - row_max[:, :, None])
    start_state = (
        jnp.sum(fresh_exp, axis=2),
        jnp.einsum(
            "thu,uc->thc",
            fresh_exp.astype(jnp.bfloat16),
            fresh_pair[:, head_dim:],
            preferred_element_type=jnp.float32,
        ),
    )
    row_total, weighted = lax.fori_loop(0, live_blocks, add_block, start_state)
    head_out = (weighted / row_total[:, :, None]).astype(jnp.bfloat16).reshape(suffix_len, -1)
    gate_weights = route_probs / jnp.sum(route_probs, axis=1, keepdims=True)
    chosen = expert_ids[:, :, None] == jnp.arange(experts_all, dtype=jnp.int32)
    gate_table = jnp.sum(jnp.where(chosen, gate_weights[:, :, None], 0.0), axis=1)
    gate_tables = [gate_table]
    for step in range(1, n_expert):
        pairs = [(source, (source + step) % n_expert) for source in range(n_expert)]
        gate_tables.append(lax.ppermute(gate_table, "expert", pairs))
    from_order = lax.rem(expert_index - jnp.arange(n_expert) + n_expert, n_expert)
    gate_all = jnp.stack(gate_tables)[from_order].reshape(n_expert * suffix_len, experts_all)
    my_expert = owner_index // share_count
    my_gates = lax.dynamic_slice_in_dim(gate_all, my_expert, 1, 1)

    seqs_each = n_expert // n_donor
    width = model_width // n_expert
    hidden_parts = []
    for shift in range(seqs_each):
        pairs = []
        for source in range(n_expert * n_donor):
            seq, part = source // n_donor, source % n_donor
            target = part * seqs_each + (seq + shift) % seqs_each
            pairs.append((source, target * n_donor + seq // seqs_each))
        target = donor_index * seqs_each + lax.rem(expert_index + shift, seqs_each)
        sent = lax.dynamic_slice_in_dim(hidden_in, target * width, width, 1)
        hidden_parts.append(lax.ppermute(sent, ("expert", "donor"), pairs))
    turned = lax.rem(expert_index - jnp.arange(seqs_each) + seqs_each * n_expert, seqs_each)
    hidden_block = jnp.stack(hidden_parts)[turned].reshape(seqs_each * suffix_len, width)

    heads_all = lax.all_gather(head_out, "expert", axis=0, tiled=True)
    w_in, heads_all = lax.optimization_barrier(
        (w_gate_up[0].reshape(model_width, 2 * ff_local), heads_all)
    )
    resid = gather_blocks(heads_all, out_weight, hidden_block, n_expert // 2, n_donor)
    resid_f = resid.astype(jnp.float32)
    inverse = lax.rsqrt(jnp.mean(resid_f * resid_f, axis=1, keepdims=True) + 1e-06)
    normed = (resid_f * inverse * norm_gain.astype(jnp.float32)).astype(jnp.bfloat16)
    gate_up = jnp.dot(
        normed,
        w_in,
        preferred_element_type=jnp.float32,
    )
    activated = (
        jax.nn.silu(gate_up[:, :ff_local]) * gate_up[:, ff_local:] * my_gates
    ).astype(jnp.bfloat16)
    expert_mix = reduce_blocks(activated, w_down[0], n_expert // 2, n_donor)
    resid_mine = lax.dynamic_slice(
        resid,
        (expert_index * suffix_len, donor_index * columns),
        (suffix_len, columns),
    )
    layer_out = (resid_mine.astype(jnp.float32) + expert_mix).astype(
        jnp.bfloat16
    )
    return (layer_out, head_out)


def solution(mesh):
    in_specs = (
        P(("groups", "expert"), None),
        P(("groups", "expert"), "donor"),
        P(("groups", "expert"), None, None),
        P(("groups", "expert", "donor"), None, None, None),
        P("groups", None),
        P("groups"),
        P("donor", "expert"),
        P(),
        P(("groups", "expert"), None),
        P(("groups", "expert"), None),
        P(("expert", "donor"), None, None, None),
        P(("expert", "donor"), None, None),
    )
    out_specs = (P(("groups", "expert"), "donor"), P(("groups", "expert"), "donor"))
    return jax.shard_map(shards, mesh=mesh, in_specs=in_specs, out_specs=out_specs, check_vma=False)
```

profile of v0, /device:TPU:0, one launch (start us, length us, event | category | flops | bytes accessed | tf_op | source)
XLA Modules:
  0.0 190.1 jit_solution(7661640148267389322)
XLA Ops:
  7.2 0.9 fusion.22
  8.4 1.5 gather_fusion
  9.9 0.8 broadcast_select_fusion
  10.7 7.4 %all-to-all-start = ((bf16[16,32,256]{2,1,0:T(8,128)(2,1)}), bf16[16,32,256]{2,1,0:T(8,128)(2,1)S(1)}, u32[]{:S(2)}, u32[]{:S(2)}) async-start(bf16[16,32,256]{2,1,0:T(8,128)(2,1)} %broadcast_select_fusion), calls=%async_computation | async-start | bytes 524288 | tf_op jit(solution)/shard_map/all_to_all | solution.py:410
  18.2 1.0 constant_dynamic-slice_fusion.3
  19.3 1.3 dynamic_slice.25
  22.1 5.7 %all-to-all-done = bf16[16,32,256]{2,1,0:T(8,128)(2,1)S(1)} async-done(((bf16[16,32,256]{2,1,0:T(8,128)(2,1)}), bf16[16,32,256]{2,1,0:T(8,128)(2,1)S(1)}, u32[]{:S(2)}, u32[]{:S(2)}) %all-to-all-start) | async-done | bytes 262176 | tf_op jit(solution)/shard_map/all_to_all | solution.py:410
  28.6 1.2 while.22
  28.6 0.7 add_compare_fusion.4
  30.3 1.9 %while.23 = (s32[]{:T(128)}, f32[128,8]{0,1:T(8,128)S(1)}, f32[128,8,128]{2,0,1:T(8,128)S(1)}, s32[]{:T(128)}, s32[]{:T(128)}, /*index=5*/bf16[128,8,128]{2,0,1:...) while((s32[]{:T(128)}, f32[128,8]{0,1:T(8,128)S(1)}, ...), condition=%wide.region_8.9_spmd, body=%wide.region_6.8_spmd.sunk | while | flops 271188992 | bytes 3691649 | solution.py:466
  30.3 0.7 add_compare_fusion.5
  31.0 0.7 fusion.48
  32.2 0.9 copy_bitcast_fusion
  33.3 1.1 collective-permute-start.2
  34.4 0.9 collective-permute-start.3
  35.3 0.7 collective-permute-start
  36.0 13.1 %copy.47 = bf16[512,8,2,768]{3,1,2,0:T(8,128)(2,1)} copy(bf16[512,8,2,768]{3,2,1,0:T(2,128)(2,1)} %bitcast.73) | data formatting | bytes 25165824
  50.5 0.7 copy-done.3
  51.2 67.8 %gather_blocks.1 = bf16[512,4096]{1,0:T(8,128)(2,1)} custom-call(bf16[512,1024]{1,0:T(8,128)(2,1)} %all-gather.2.cloned.1.call-done.heads_ref, bf16[1024,1024]{1,0:T(8,128)(2,1)} %out_ref.1, bf16[128,1024]{1,0:T(8,128)(2,1)} %copy-done.3), custom_call_target="tpu_custom_call" | custom-call | tf_op jit(solution)/shard_map/gather_blocks/pallas_call | solution.py:195
  119.0 3.2 %fusion.4 = f32[512]{0:T(512)S(1)} fusion(bf16[512,4096]{1,0:T(8,128)(2,1)} %gather_blocks.1), kind=kLoop, calls=%fused_computation.14 | loop fusion | flops 6290944 | bytes 4196352 | tf_op jit(solution)/shard_map/reduce_sum | solution.py:501
  122.4 9.5 %fusion.7 = f32[512,1536]{1,0:T(8,128)S(1)} fusion(bf16[4096,1536]{1,0:T(8,128)(2,1)} %bitcast.74, bf16[512,4096]{1,0:T(8,128)(2,1)S(1)} %copy-done.1, f32[4096]{0:T(1024)S(1)} %convert_element_type.31, f32[512]{0:T(512)S(1)} %add_rsqrt_fusion), kind=kOutput, calls=%fused_computation.17 | convolution fusion | flops 6450839552 | bytes 19941376 | tf_op jit(solution)/shard_map/dot_general | solution.py:503
  131.9 1.3 fusion.12.act_ref
  133.3 48.1 %reduce_blocks.1 = f32[128,1024]{1,0:T(8,128)} custom-call(bf16[512,768]{1,0:T(8,128)(2,1)} %fusion.12.act_ref, bf16[768,4096]{1,0:T(8,128)(2,1)} %bitcast.75), custom_call_target="tpu_custom_call" | custom-call | tf_op jit(solution)/shard_map/reduce_blocks/pallas_call | solution.py:349
  181.4 1.9 add_convert_fusion
  (58 shorter events, 4.8 us)
Async XLA Ops:
  7.2 28.1 %copy-start = (bf16[128,4096]{1,0:T(8,128)(2,1)S(1)}, bf16[128,4096]{1,0:T(8,128)(2,1)}, u32[]{:S(2)}) copy-start(bf16[128,4096]{1,0:T(8,128)(2,1)} %param.16) | copy-start | bytes 3145732
  7.2 14.1 %copy-start.2 = (bf16[128,1024]{1,0:T(8,128)(2,1)S(1)}, bf16[128,1024]{1,0:T(8,128)(2,1)}, u32[]{:S(2)}) copy-start(bf16[128,1024]{1,0:T(8,128)(2,1)} %param.17) | copy-start | bytes 786436
  10.7 17.2 %all-to-all-start = ((bf16[16,32,256]{2,1,0:T(8,128)(2,1)}), bf16[16,32,256]{2,1,0:T(8,128)(2,1)S(1)}, u32[]{:S(2)}, u32[]{:S(2)}) async-start(bf16[16,32,256]{2,1,0:T(8,128)(2,1)} %broadcast_select_fusion), calls=%async_computation | async-start | bytes 524288 | tf_op jit(solution)/shard_map/all_to_all | solution.py:410
  18.1 32.3 %all-gather.2.cloned.1.call-start = ((), (), s32[]{:S(2)}) async-start(), calls=%async_computation.1 | async-start | bytes 1310720 | tf_op jit(solution)/shard_map/all_gather | solution.py:495
  30.3 2.9 %copy-start.5 = (f32[128,4]{0,1:T(4,128)S(1)}, f32[128,4]{0,1:T(4,128)}, u32[]{:S(2)}) copy-start(f32[128,4]{0,1:T(4,128)} %param.25) | copy-start | bytes 6148
  30.3 2.9 %copy-start.6 = (s32[128,4]{0,1:T(4,128)S(1)}, s32[128,4]{0,1:T(4,128)}, u32[]{:S(2)}) copy-start(s32[128,4]{0,1:T(4,128)} %param.24) | copy-start | bytes 6148
  33.2 16.0 %collective-permute-start.1 = (f32[128,8]{0,1:T(8,128)S(1)}, f32[128,8]{0,1:T(8,128)S(1)}, u32[]{:S(2)}, u32[]{:S(2)}) collective-permute-start(f32[128,8]{0,1:T(8,128)S(1)} %select_reduce_fusion.1), channel_id=1, source_target_pairs={{0,4},{4,8},{8,12},{12,0},{1,5},{5,9},{9,13},{13,1},{2,6},{6,10},{... | collective-permute-start | bytes 12296 | tf_op jit(solution)/shard_map/ppermute | solution.py:474
  33.3 15.9 %collective-permute-start.2 = (f32[128,8]{0,1:T(8,128)S(1)}, f32[128,8]{0,1:T(8,128)S(1)}, u32[]{:S(2)}, u32[]{:S(2)}) collective-permute-start(f32[128,8]{0,1:T(8,128)S(1)} %select_reduce_fusion.1), channel_id=1, source_target_pairs={{0,8},{4,12},{8,0},{12,4},{1,9},{5,13},{9,1},{13,5},{2,10},{6,14},... | collective-permute-start | bytes 12296 | tf_op jit(solution)/shard_map/ppermute | solution.py:474
  34.4 14.8 %collective-permute-start.3 = (f32[128,8]{0,1:T(8,128)S(1)}, f32[128,8]{0,1:T(8,128)S(1)}, u32[]{:S(2)}, u32[]{:S(2)}) collective-permute-start(f32[128,8]{0,1:T(8,128)S(1)} %select_reduce_fusion.1), channel_id=1, source_target_pairs={{0,12},{4,0},{8,4},{12,8},{1,13},{5,1},{9,5},{13,9},{2,14},{6,2},{... | collective-permute-start | bytes 12296 | tf_op jit(solution)/shard_map/ppermute | solution.py:474
  35.3 15.2 %collective-permute-start = (bf16[128,1024]{1,0:T(8,128)(2,1)S(1)}, bf16[128,1024]{1,0:T(8,128)(2,1)S(1)}, u32[]{:S(2)}, u32[]{:S(2)}) collective-permute-start(bf16[128,1024]{1,0:T(8,128)(2,1)S(1)} %constant_dynamic-slice_fusion.1), channel_id=1, source_target_pairs={{0,0},{1,4},{2,8},{3,12},{4,1},{5,5},{6,9},{7,13},{8,2},{9,6},{10,... | collective-permute-start | bytes 786440 | tf_op jit(solution)/shard_map/ppermute | solution.py:491
  36.0 13.2 %copy-start.4 = (bf16[4096]{0:T(1024)(128)(2,1)S(1)}, bf16[4096]{0:T(1024)(128)(2,1)}, u32[]{:S(2)}) copy-start(bf16[4096]{0:T(1024)(128)(2,1)} %param.23) | copy-start | bytes 24580
  50.5 0.7 copy-start.3
  119.0 3.5 %copy-start.1 = (bf16[512,4096]{1,0:T(8,128)(2,1)S(1)}, bf16[512,4096]{1,0:T(8,128)(2,1)}, u32[]{:S(2)}) copy-start(bf16[512,4096]{1,0:T(8,128)(2,1)} %gather_blocks.1) | copy-start | bytes 12582916
Sparse Core Ops, SparseCore 0:
  33.2 17.1 all-gather.1
where the time goes:
time: 191 us; the launch traced here: 190 us
  Pallas kernels  116 us (61%)
  local copies, waits for them, and re-layouts  19.8 us (10%)
  between operations  15.1 us (8%)
  matrix products  11.6 us (6%)
  other arithmetic  10.9 us (6%)
  starting transfers between devices  10.2 us (5%)
  waiting for transfers between devices  6.42 us (3%)
    pallas_call x1, Pallas kernels, gather_blocks(): pl.pallas_call(functools.partial(gather_kernel, chips, donors), out_shape...  67.8 us
    pallas_call x1, Pallas kernels, reduce_blocks(): pl.pallas_call(functools.partial(reduce_kernel, chips, donors), out_shape...  48.1 us
    unnamed x17, local copies, waits for them, and re-layouts  14.3 us
    dot_general x1, matrix products, shards(): gate_up = jnp.dot(normed, w_in, preferred_element_type=jnp.float32)  9.47 us
    all_to_all x1, starting transfers between devices, shards(): lax.all_to_all(outgoing, ('expert', 'donor'), split_axis=0, concat_axis=0...  7.41 us
    all_to_all x1, waiting for transfers between devices, shards(): lax.all_to_all(outgoing, ('expert', 'donor'), split_axis=0, concat_axis=0...  5.74 us
  transfers between devices with their start and end apart: 6, of which 2 were waited for; matrix products, arithmetic and copies ran while one was open for 9% of the time, Pallas kernels for 0%

commit v1 on v0

--- a/solution.py
+++ b/solution.py
@@ -1,4 +1,5 @@
 import functools
+import math
 
 import jax
 import jax.numpy as jnp
@@ -8,6 +9,8 @@
 from jax.sharding import PartitionSpec as P
 
 MESH = pl.DeviceIdType.MESH
+VMEM_BYTES = 60 * 1024 * 1024
+PIECE = 64
 
 
 def place():
@@ -368,6 +371,642 @@
         compiler_params=pltpu.CompilerParams(collective_id=2, has_side_effects=True),
         name="reduce_blocks",
     )(activated, down)
+
+
+def mix_kernel(
+    chips,
+    donors,
+    piece,
+    heads_in,
+    hidden_ref,
+    gain_ref,
+    gates_ref,
+    outw_hbm,
+    raw_hbm,
+    down_hbm,
+    out_ref,
+    outw_ref,
+    raw_ref,
+    down_ref,
+    heads_ref,
+    p_ref,
+    r_out,
+    r_in,
+    l_out,
+    l_in,
+    full_ref,
+    w_ref,
+    x_ref,
+    acc_ref,
+    ssq_ref,
+    act_ref,
+    part_ref,
+    c_in,
+    y_out,
+    y_in,
+    zr_out,
+    zr_in,
+    zl_out,
+    zl_in,
+    local_sem,
+    raw_sem,
+    hy_send,
+    hy_recv,
+    hc_send,
+    hc_recv,
+    r_send,
+    r_recv,
+    l_send,
+    l_recv,
+    y_send,
+    y_recv,
+    c_send,
+    c_recv,
+    cc_send,
+    cc_recv,
+    yy_send,
+    yy_recv,
+    zr_send,
+    zr_recv,
+    zl_send,
+    zl_recv,
+):
+    row, core, donor = place()
+    mine = row * 2 + core
+    beside = row * 2 + 1 - core
+    suffix, head_cols = heads_in.shape
+    blocks, tokens, width = full_ref.shape
+    model_width, ff_both = w_ref.shape
+    ff_local = ff_both // 2
+    seqs_each = hidden_ref.shape[0] // suffix
+    per_seq = suffix // piece
+    count = blocks * per_seq
+    per_group = count // chips
+    group_rows = 2 * suffix
+    columns = out_ref.shape[1]
+    last = donors - 1
+    lag = 2
+    first_mix = per_group + lag
+    raw_steps, raw_slots, raw_rows = raw_sem.shape[0], raw_ref.shape[0], raw_ref.shape[1]
+    relay = min(128, raw_rows)
+    strip = 16
+
+    own_copies = [
+        pltpu.make_async_copy(outw_hbm, outw_ref, local_sem.at[0]),
+        pltpu.make_async_copy(heads_in, heads_ref.at[pl.ds(mine * suffix, suffix)], local_sem.at[1]),
+        pltpu.make_async_copy(down_hbm.at[0], down_ref, local_sem.at[2]),
+    ]
+    own_copies[0].start()
+    own_copies[1].start()
+
+    def raw_copy(index):
+        at = pl.ds(pl.multiple_of(index * raw_rows, raw_rows), raw_rows)
+        return pltpu.make_async_copy(
+            raw_hbm.at[0, at], raw_ref.at[lax.rem(index, raw_slots)], raw_sem.at[index]
+        )
+
+    for index in range(raw_slots):
+        raw_copy(index).start()
+    own_copies[2].start()
+
+    barrier = pltpu.get_barrier_semaphore()
+    pl.semaphore_signal(barrier, inc=1, device_id={"expert": beside}, device_id_type=MESH)
+    for step in range(1, chips):
+        other = lax.rem(row + step, chips) * 2 + core
+        pl.semaphore_signal(barrier, inc=1, device_id={"expert": other}, device_id_type=MESH)
+
+    @pl.when(donor > 0)
+    def _():
+        pl.semaphore_signal(barrier, inc=1, device_id={"donor": donor - 1}, device_id_type=MESH)
+
+    @pl.when(donor < last)
+    def _():
+        pl.semaphore_signal(barrier, inc=1, device_id={"donor": donor + 1}, device_id_type=MESH)
+
+    acc_ref[...] = jnp.zeros_like(acc_ref)
+    ssq_ref[...] = jnp.zeros_like(ssq_ref)
+    pl.semaphore_wait(barrier, chips + jnp.minimum(donor, 1) + jnp.minimum(last - donor, 1))
+
+    def heads_of(seq):
+        return heads_ref.at[pl.ds(pl.multiple_of(seq * suffix, suffix), suffix)]
+
+    def heads_y(step, seq, to):
+        return send(heads_of(seq), heads_of(seq), hy_send, hy_recv, step - 1, expert=to)
+
+    def heads_c(slot, seq):
+        return send(heads_of(seq), heads_of(seq), hc_send, hc_recv, slot, expert=beside)
+
+    own_copies[1].wait()
+    heads_c(0, mine).start()
+    for step in range(1, chips):
+        heads_y(step, mine, lax.rem(row + step, chips) * 2 + core).start()
+    own_copies[0].wait()
+
+    def seq_at(from_row, from_core, index):
+        return lax.rem(from_row + index // 2, chips) * 2 + lax.rem(from_core + lax.rem(index, 2), 2)
+
+    def tile(from_row, from_core, chunk):
+        seq = seq_at(from_row, from_core, chunk // per_seq)
+        top = pl.multiple_of(seq * suffix + lax.rem(chunk, per_seq) * piece, piece)
+        return full_ref.at[from_row * 2 + from_core, pl.ds(top, piece)]
+
+    def right(chunk):
+        return send(r_out.at[chunk], r_in.at[chunk], r_send, r_recv, chunk, donor=donor + 1)
+
+    def left(chunk):
+        return send(l_out.at[chunk], l_in.at[chunk], l_send, l_recv, chunk, donor=donor - 1)
+
+    def across(step, chunk, from_row, to):
+        there = tile(from_row, core, chunk)
+        return send(there, there, y_send, y_recv, (step - 1) * count + chunk, expert=to)
+
+    def over(step, chunk, from_row, from_core):
+        there = tile(from_row, from_core, chunk)
+        return send(there, there, c_send, c_recv, step * count + chunk, expert=beside)
+
+    reach = jnp.maximum(donor, last - donor)
+
+    def partial(index):
+        seq = seq_at(row, core, index)
+        step = index // 2
+
+        @pl.when((index > 0) & (lax.rem(index, 2) == 0))
+        def _():
+            back = lax.rem(chips - step, chips)
+            copy = send(
+                heads_of(seq), heads_of(seq), hy_send, hy_recv, back - 1, expert=beside
+            )
+            copy.wait_recv()
+            heads_c(back, seq).start()
+
+        @pl.when(lax.rem(index, 2) == 1)
+        def _():
+            heads_c(lax.rem(chips - step, chips), seq).wait_recv()
+
+        at = pl.ds(pl.multiple_of(index * suffix, suffix), suffix)
+        p_ref[at, :] = jnp.dot(
+            heads_ref[pl.ds(pl.multiple_of(seq * suffix, suffix), suffix), :],
+            outw_ref[...],
+            preferred_element_type=jnp.float32,
+        )
+
+        @pl.when(seq // seqs_each == donor)
+        def _():
+            top = pl.multiple_of(lax.rem(seq, seqs_each) * suffix, suffix)
+            p_ref[at, :] = p_ref[at, :] + hidden_ref[pl.ds(top, suffix), :].astype(jnp.float32)
+
+    def p_rows(chunk):
+        return p_ref[pl.ds(pl.multiple_of(chunk * piece, piece), piece), :]
+
+    def relay_weights(index):
+        raw_copy(index).wait()
+        half = lax.broadcasted_iota(jnp.int32, (relay, 2 * relay), 0)
+        whole = lax.broadcasted_iota(jnp.int32, (relay, 2 * relay), 1)
+
+        def body(part, carry):
+            at = pl.ds(pl.multiple_of(index * raw_rows + part * relay, relay), relay)
+            from_at = pl.ds(pl.multiple_of(part * relay, relay), relay)
+            both = raw_ref[lax.rem(index, raw_slots), from_at].reshape(2 * relay, ff_local)
+            for side in range(2):
+                pick = (whole == 2 * half + side).astype(raw_ref.dtype)
+                w_ref[at, side * ff_local : (side + 1) * ff_local] = jnp.dot(
+                    pick, both, preferred_element_type=jnp.float32
+                ).astype(w_ref.dtype)
+            return carry
+
+        lax.fori_loop(0, raw_rows // relay, body, 0)
+
+        @pl.when(index + raw_slots < raw_steps)
+        def _():
+            raw_copy(index + raw_slots).start()
+
+    cut = ff_both // 3
+
+    def mix(turn, index):
+        from_row = lax.rem(row + index // 2, chips)
+        from_core = lax.rem(core + lax.rem(index, 2), 2)
+        back = lax.rem(chips - index // 2, chips)
+
+        @pl.when(lax.rem(index, 2) == 1)
+        def _():
+            def body(chunk, carry):
+                over(back, turn * per_group + chunk, from_row, from_core).wait_recv()
+                return carry
+
+            lax.fori_loop(0, per_group, body, 0)
+
+        block = from_row * 2 + from_core
+        group = lax.rem(from_row + turn, chips)
+        top = pl.multiple_of(group * group_rows, group_rows)
+        left_at = pl.multiple_of(block * width, width)
+        gain = gain_ref[:, pl.ds(left_at, width)].astype(jnp.float32)
+
+        def scale(part, carry):
+            here = pl.ds(pl.multiple_of(part * strip, strip), strip)
+            at = pl.ds(pl.multiple_of(top + part * strip, strip), strip)
+            value = full_ref[block, at, :].astype(jnp.float32)
+            x_ref[here, :] = (value * gain).astype(x_ref.dtype)
+            square = value * value
+            total = square[:, :128]
+            for start in range(128, width, 128):
+                total = total + square[:, start : start + 128]
+            ssq_ref[at, :] = ssq_ref[at, :] + total
+            return carry
+
+        lax.fori_loop(0, group_rows // strip, scale, 0)
+        at = pl.ds(top, group_rows)
+
+        def multiply(part, carry):
+            wide = pl.ds(pl.multiple_of(part * cut, cut), cut)
+            acc_ref[at, wide] = acc_ref[at, wide] + jnp.dot(
+                x_ref[...], w_ref[pl.ds(left_at, width), wide], preferred_element_type=jnp.float32
+            )
+            return carry
+
+        lax.fori_loop(0, ff_both // cut, multiply, 0)
+
+    early = blocks * (chips - 1)
+
+    def march(t, carry):
+        @pl.when((t < count) & (lax.rem(t, per_seq) == 0))
+        def _():
+            partial(t // per_seq)
+
+        here = t - donor
+
+        @pl.when((here >= 0) & (here < count))
+        def _():
+            @pl.when(donor == 0)
+            def _():
+                r_out[here] = p_rows(here).astype(r_out.dtype)
+
+            @pl.when(donor > 0)
+            def _():
+                right(here).wait_recv()
+
+            @pl.when((donor > 0) & (donor < last))
+            def _():
+                r_out[here] = (p_rows(here) + r_in[here].astype(jnp.float32)).astype(r_out.dtype)
+
+            @pl.when(donor < last)
+            def _():
+                right(here).start()
+
+        there = t - (last - donor)
+
+        @pl.when((there >= 0) & (there < count))
+        def _():
+            @pl.when(donor == last)
+            def _():
+                l_out[there] = p_rows(there).astype(l_out.dtype)
+
+            @pl.when(donor < last)
+            def _():
+                left(there).wait_recv()
+
+            @pl.when((donor > 0) & (donor < last))
+            def _():
+                l_out[there] = (p_rows(there) + l_in[there].astype(jnp.float32)).astype(l_out.dtype)
+
+            @pl.when(donor > 0)
+            def _():
+                left(there).start()
+
+        done = t - reach
+
+        @pl.when((done >= 0) & (done < count))
+        def _():
+            goal = tile(row, core, done)
+
+            @pl.when(donor == 0)
+            def _():
+                goal[...] = (p_rows(done) + l_in[done].astype(jnp.float32)).astype(goal.dtype)
+
+            @pl.when(donor == last)
+            def _():
+                goal[...] = (p_rows(done) + r_in[done].astype(jnp.float32)).astype(goal.dtype)
+
+            @pl.when((donor > 0) & (donor < last))
+            def _():
+                goal[...] = (
+                    p_rows(done) + r_in[done].astype(jnp.float32) + l_in[done].astype(jnp.float32)
+                ).astype(goal.dtype)
+
+            for step in range(1, chips):
+                across(step, done, row, lax.rem(row + step, chips) * 2 + core).start()
+            over(0, done, row, core).start()
+
+        came = t - reach - lag
+
+        @pl.when((came >= 0) & (came < count))
+        def _():
+            for step in range(1, chips):
+                from_row = lax.rem(row + chips - step, chips)
+                across(step, came, from_row, from_row * 2 + core).wait_recv()
+                over(step, came, from_row, core).start()
+
+        @pl.when(t < raw_steps)
+        def _():
+            relay_weights(t)
+
+        ready = t - reach - first_mix
+
+        @pl.when((ready >= 0) & (ready < early))
+        def _():
+            mix(ready // blocks, lax.rem(ready, blocks))
+
+        return carry
+
+    steps = count + last + lag
+    lax.fori_loop(0, steps, march, 0)
+
+    def rest(index, carry):
+        mix(index // blocks, lax.rem(index, blocks))
+        return carry
+
+    lax.fori_loop(jnp.minimum(steps - reach - first_mix, early), early, rest, 0)
+    own_copies[2].wait()
+
+    def activate(group):
+        def body(part, carry):
+            at = pl.ds(pl.multiple_of(group * group_rows + part * strip, strip), strip)
+            mean = jnp.sum(ssq_ref[at, :], axis=1, keepdims=True) * (1.0 / model_width)
+            inverse = lax.rsqrt(mean + 1e-06)
+            gate = acc_ref[at, :ff_local] * inverse
+            up = acc_ref[at, ff_local:] * inverse
+            value = gate / (1.0 + jnp.exp(-gate)) * up * gates_ref[at, :]
+            act_ref[at, :] = value.astype(act_ref.dtype)
+            return carry
+
+        lax.fori_loop(0, group_rows // strip, body, 0)
+
+    def target(rank):
+        low = jnp.minimum(donor, last - donor)
+        single = reach - low
+        rest_rank = rank - single
+        gap = low - rest_rank // 2
+        side = 1 - 2 * lax.rem(jnp.maximum(rest_rank, 0), 2)
+        paired = donor + side * gap
+        lone = jnp.where(donor < last - donor, last - rank, rank)
+        return jnp.where(rank == last, donor, jnp.where(rank < single, lone, paired))
+
+    def add(out, *terms):
+        def body(part, carry):
+            at = pl.ds(pl.multiple_of(part * strip, strip), strip)
+            value = terms[0][at, :].astype(jnp.float32)
+            for term in terms[1:]:
+                value = value + term[at, :].astype(jnp.float32)
+            out[at, :] = value.astype(out.dtype)
+            return carry
+
+        lax.fori_loop(0, suffix // strip, body, 0)
+
+    order = list(range(1, chips)) + [0]
+
+    def own_half(slot):
+        return part_ref.at[slot, pl.ds(pl.multiple_of(core * suffix, suffix), suffix)]
+
+    def swap(slot):
+        away = part_ref.at[slot, pl.ds(pl.multiple_of((1 - core) * suffix, suffix), suffix)]
+        return send(away, c_in.at[slot], cc_send, cc_recv, slot, expert=beside)
+
+    def cross(hop, to):
+        return send(y_out.at[hop], y_in.at[hop], yy_send, yy_recv, hop, expert=to)
+
+    def produce(step, rank):
+        slot = step * donors + rank
+        top = pl.multiple_of(lax.rem(row + step, chips) * group_rows, group_rows)
+        left_at = pl.multiple_of(target(rank) * columns, columns)
+        part_ref[slot] = jnp.dot(
+            act_ref[pl.ds(top, group_rows), :],
+            down_ref[:, pl.ds(left_at, columns)],
+            preferred_element_type=jnp.float32,
+        ).astype(part_ref.dtype)
+        swap(slot).start()
+
+    def pass_on(step, rank):
+        slot = step * donors + rank
+        hop = (step - 1) * donors + rank
+        swap(slot).wait_recv()
+        add(y_out.at[hop], own_half(slot), c_in.at[slot])
+        cross(hop, lax.rem(row + step, chips) * 2 + core).start()
+
+    for step in order:
+        for side in range(2):
+            mix(chips - 1, 2 * ((step + 1) % chips) + side)
+        activate(lax.rem(row + step, chips))
+        if step:
+
+            def body(rank, carry):
+                produce(step, rank)
+
+                @pl.when(rank > 0)
+                def _():
+                    pass_on(step, rank - 1)
+
+                return carry
+
+            lax.fori_loop(0, donors, body, 0)
+            pass_on(step, donors - 1)
+        else:
+
+            def body(rank, carry):
+                produce(0, rank)
+                return carry
+
+            lax.fori_loop(0, donors, body, 0)
+
+    def shift_right(goal):
+        return send(zr_out.at[goal], zr_in.at[goal], zr_send, zr_recv, goal, donor=donor + 1)
+
+    def shift_left(goal):
+        return send(zl_out.at[goal], zl_in.at[goal], zl_send, zl_recv, goal, donor=donor - 1)
+
+    def finish(rank, carry):
+        goal = target(rank)
+        swap(rank).wait_recv()
+        terms = [own_half(rank), c_in.at[rank]]
+        for step in range(1, chips):
+            hop = (step - 1) * donors + rank
+            cross(hop, mine).wait_recv()
+            terms.append(y_in.at[hop])
+
+        @pl.when((goal >= donor) & (donor > 0))
+        def _():
+            shift_right(goal).wait_recv()
+
+        @pl.when((goal <= donor) & (donor < last))
+        def _():
+            shift_left(goal).wait_recv()
+
+        @pl.when(goal > donor)
+        def _():
+            @pl.when(donor == 0)
+            def _():
+                add(zr_out.at[goal], *terms)
+
+            @pl.when(donor > 0)
+            def _():
+                add(zr_out.at[goal], zr_in.at[goal], *terms)
+
+            shift_right(goal).start()
+
+        @pl.when(goal < donor)
+        def _():
+            @pl.when(donor == last)
+            def _():
+                add(zl_out.at[goal], *terms)
+
+            @pl.when(donor < last)
+            def _():
+                add(zl_out.at[goal], zl_in.at[goal], *terms)
+
+            shift_left(goal).start()
+
+        @pl.when(goal == donor)
+        def _():
+            def close(ends):
+                for part in range(columns // width):
+                    wide = slice(part * width, (part + 1) * width)
+
+                    def body(index, carry):
+                        at = pl.ds(pl.multiple_of(index * strip, strip), strip)
+                        down = pl.ds(pl.multiple_of(mine * suffix + index * strip, strip), strip)
+                        value = full_ref[donor * (columns // width) + part, down, :].astype(jnp.float32)
+                        total = terms[0][at, wide].astype(jnp.float32)
+                        for term in terms[1:] + ends:
+                            total = total + term[at, wide].astype(jnp.float32)
+                        out_ref[at, wide] = (value + total).astype(out_ref.dtype)
+                        return carry
+
+                    lax.fori_loop(0, suffix // strip, body, 0)
+
+            @pl.when(donor == 0)
+            def _():
+                close([zl_in.at[donor]])
+
+            @pl.when(donor == last)
+            def _():
+                close([zr_in.at[donor]])
+
+            @pl.when((donor > 0) & (donor < last))
+            def _():
+                close([zl_in.at[donor], zr_in.at[donor]])
+
+        return carry
+
+    lax.fori_loop(0, donors, finish, 0)
+
+    for step in range(1, chips):
+        heads_y(step, mine, mine).wait_send()
+    for step in range(chips):
+        heads_c(step, mine).wait_send()
+
+    def drain(chunk, carry):
+        @pl.when(donor < last)
+        def _():
+            right(chunk).wait_send()
+
+        @pl.when(donor > 0)
+        def _():
+            left(chunk).wait_send()
+
+        for step in range(1, chips):
+            across(step, chunk, row, mine).wait_send()
+        for step in range(chips):
+            over(step, chunk, row, core).wait_send()
+        return carry
+
+    lax.fori_loop(0, count, drain, 0)
+
+    def drain_blocks(goal, carry):
+        for step in range(chips):
+            swap(step * donors + goal).wait_send()
+        for step in range(1, chips):
+            cross((step - 1) * donors + goal, mine).wait_send()
+
+        @pl.when(goal > donor)
+        def _():
+            shift_right(goal).wait_send()
+
+        @pl.when(goal < donor)
+        def _():
+            shift_left(goal).wait_send()
+
+        return carry
+
+    lax.fori_loop(0, donors, drain_blocks, 0)
+
+
+def mix_scratch(heads, out_weight, w_gate_up, chips, donors, piece):
+    suffix, head_cols = heads.shape
+    blocks = 2 * chips
+    width = out_weight.shape[1]
+    model_width, ff_local = w_gate_up.shape[1], w_gate_up.shape[3]
+    tokens = blocks * suffix
+    columns = model_width // donors
+    count = tokens // piece
+    kind = heads.dtype
+    vmem = lambda *shape: pltpu.VMEM(shape, kind)
+    wide = lambda *shape: pltpu.VMEM(shape, jnp.float32)
+    held = lambda number: pltpu.VMEM((number, suffix, columns), kind)
+    return [
+        vmem(head_cols, width),
+        vmem(3, model_width // 8, 2, ff_local),
+        vmem(ff_local, model_width),
+        vmem(tokens, head_cols),
+        wide(tokens, width),
+        vmem(count, piece, width),
+        vmem(count, piece, width),
+        vmem(count, piece, width),
+        vmem(count, piece, width),
+        vmem(blocks, tokens, width),
+        vmem(model_width, 2 * ff_local),
+        vmem(2 * suffix, width),
+        wide(tokens, 2 * ff_local),
+        wide(tokens, 128),
+        vmem(tokens, ff_local),
+        vmem(chips * donors, 2 * suffix, columns),
+        held(chips * donors),
+        held((chips - 1) * donors),
+        held((chips - 1) * donors),
+        held(donors),
+        held(donors),
+        held(donors),
+        held(donors),
+    ]
+
+
+def mix_blocks(heads, hidden, gain, gates, out_weight, w_gate_up, w_down, chips, donors, piece, scratch):
+    suffix = heads.shape[0]
+    columns = w_gate_up.shape[1] // donors
+    count = 2 * chips * suffix // piece
+    dma = pltpu.SemaphoreType.DMA
+    pair = lambda number: [dma((number,)), dma((number,))]
+    inside = pl.BlockSpec(memory_space=pltpu.VMEM)
+    outside = pl.BlockSpec(memory_space=pl.ANY)
+    return pl.pallas_call(
+        functools.partial(mix_kernel, chips, donors, piece),
+        out_shape=jax.ShapeDtypeStruct((suffix, columns), heads.dtype),
+        in_specs=[inside] * 4 + [outside] * 3,
+        out_specs=inside,
+        scratch_shapes=scratch
+        + [dma((3,)), dma((8,))]
+        + pair(chips - 1)
+        + pair(chips)
+        + pair(count)
+        + pair(count)
+        + pair((chips - 1) * count)
+        + pair(chips * count)
+        + pair(chips * donors)
+        + pair((chips - 1) * donors)
+        + pair(donors)
+        + pair(donors),
+        compiler_params=pltpu.CompilerParams(
+            collective_id=3, has_side_effects=True, vmem_limit_bytes=VMEM_BYTES
+        ),
+        name="mix_blocks",
+    )(heads, hidden, gain, gates, out_weight, w_gate_up, w_down)
 
 
 def shards(
@@ -492,6 +1131,25 @@
     turned = lax.rem(expert_index - jnp.arange(seqs_each) + seqs_each * n_expert, seqs_each)
     hidden_block = jnp.stack(hidden_parts)[turned].reshape(seqs_each * suffix_len, width)
 
+    chips = n_expert // 2
+    scratch = mix_scratch(head_out, out_weight, w_gate_up, chips, n_donor, PIECE)
+    held_bytes = sum(math.prod(item.shape) * item.dtype.itemsize for item in scratch)
+    if held_bytes <= VMEM_BYTES - 4 * 1024 * 1024:
+        layer_out = mix_blocks(
+            head_out,
+            hidden_block,
+            norm_gain.reshape(1, model_width),
+            my_gates,
+            out_weight,
+            w_gate_up,
+            w_down,
+            chips,
+            n_donor,
+            PIECE,
+            scratch,
+        )
+        return (layer_out, head_out)
+
     heads_all = lax.all_gather(head_out, "expert", axis=0, tiled=True)
     w_in, heads_all = lax.optimization_barrier(
         (w_gate_up[0].reshape(model_width, 2 * ff_local), heads_all)

time: 191 us -> 131 us (0.69)
  Pallas kernels: 116 us -> 98.1 us
  between operations: 15.1 us -> 1.6 us
  local copies, waits for them, and re-layouts: 19.8 us -> 8.08 us
  matrix products: 11.6 us -> 2.16 us
  other arithmetic: 10.9 us -> 6.36 us
  waiting for transfers between devices: 6.42 us -> 4.5 us
    pallas_call x2 -> x1, Pallas kernels: 116 us -> 98.1 us  [mix_blocks(): pl.pallas_call(functools.partial(mix_kernel, chips, donors, piece), out_s...]
    unnamed x17 -> x15, local copies, waits for them, and re-layouts: 14.3 us -> 2.58 us
    dot_general x1 -> x0, matrix products: 9.47 us -> none  [shards(): gate_up = jnp.dot(normed, w_in, preferred_element_type=jnp.float32)]
    reduce_sum x1 -> x0, other arithmetic: 3.23 us -> none  [shards(): jnp.mean(resid_f * resid_f, axis=1, keepdims=True) + 1e-06]
    convert_element_type x3 -> x0, other arithmetic: 3.21 us -> none  [the longest x1 1.88 us: shards(): (resid_mine.astype(jnp.float32) + expert_mix).astype(jnp.bfloat16)]
  transfers between devices with their start and end apart: 6 -> 5, of which waited for: 2 -> 1; matrix products, arithmetic and copies ran while one was open for 9% -> 9% of each run, Pallas kernels for 0% -> 0%
where the time goes in v1:
time: 131 us
  Pallas kernels  98.1 us (75%)
  starting transfers between devices  9.91 us (8%)
  local copies, waits for them, and re-layouts  8.08 us (6%)
  other arithmetic  6.36 us (5%)
  waiting for transfers between devices  4.5 us (3%)
  matrix products  2.16 us (2%)
  between operations  1.6 us (1%)
    pallas_call x1, Pallas kernels, mix_blocks(): pl.pallas_call(functools.partial(mix_kernel, chips, donors, piece), out_s...  98.1 us
    all_to_all x1, starting transfers between devices, shards(): lax.all_to_all(outgoing, ('expert', 'donor'), split_axis=0, concat_axis=0...  6 us
    all_to_all x1, waiting for transfers between devices, shards(): lax.all_to_all(outgoing, ('expert', 'donor'), split_axis=0, concat_axis=0...  4.49 us
    ppermute x3, starting transfers between devices, shards(): gate_tables.append(lax.ppermute(gate_table, 'expert', pairs))  3.23 us
  transfers between devices with their start and end apart: 5, of which 1 were waited for; matrix products, arithmetic and copies ran while one was open for 9% of the time, Pallas kernels for 0%

profile of v1, /device:TPU:0, one launch (start us, length us, event | category | flops | bytes accessed | tf_op | source)
XLA Modules:
  0.0 130.8 jit_solution(13883119023123648610)
XLA Ops:
  0.7 0.8 reduce_sum.47
  1.5 0.7 broadcast_divide_fusion
  2.2 0.7 select_reduce_fusion.1
  2.9 2.4 %collective-permute-start.3 = (f32[128,8]{0,1:T(8,128)S(1)}, f32[128,8]{0,1:T(8,128)S(1)}, u32[]{:S(2)}, u32[]{:S(2)}) collective-permute-start(f32[128,8]{0,1:T(8,128)S(1)} %select_reduce_fusion.1), channel_id=1, source_target_pairs={{0,12},{4,0},{8,4},{12,8},{1,13},{5,1},{9,5},{13,9},{2,14},{6,2},{... | collective-permute-start | bytes 12296 | tf_op jit(solution)/shard_map/ppermute | solution.py:1113
  5.3 0.6 collective-permute-start.2
  6.1 0.8 fusion.13
  7.2 1.5 %gather_fusion = bf16[16,32,256]{2,1,0:T(8,128)(2,1)S(1)} fusion(bf16[8,32,256]{2,1,0:T(8,128)(2,1)} %bitcast.70, s32[1024]{0:T(1024)S(1)} %pad_clamp_fusion.2), kind=kCustom, calls=%fused_computation | custom fusion | bytes 524352 | tf_op jit(solution)/shard_map/jit(_take)/gather | solution.py:1046
  8.7 0.8 broadcast_select_fusion
  9.5 6.0 %all-to-all-start = ((bf16[16,32,256]{2,1,0:T(8,128)(2,1)}), bf16[16,32,256]{2,1,0:T(8,128)(2,1)S(1)}, u32[]{:S(2)}, u32[]{:S(2)}) async-start(bf16[16,32,256]{2,1,0:T(8,128)(2,1)} %broadcast_select_fusion), calls=%async_computation | async-start | bytes 524288 | tf_op jit(solution)/shard_map/all_to_all | solution.py:1049
  15.5 0.7 collective-permute-start
  16.9 0.7 dynamic_slice.22
  18.6 0.6 reshape.191.gain_ref
  19.9 0.8 constant_dynamic-slice_fusion.gates_ref
  20.8 4.5 %all-to-all-done = bf16[16,32,256]{2,1,0:T(8,128)(2,1)S(1)} async-done(((bf16[16,32,256]{2,1,0:T(8,128)(2,1)}), bf16[16,32,256]{2,1,0:T(8,128)(2,1)S(1)}, u32[]{:S(2)}, u32[]{:S(2)}) %all-to-all-start) | async-done | bytes 262176 | tf_op jit(solution)/shard_map/all_to_all | solution.py:1049
  25.3 0.6 gather_fusion.1
  26.0 1.2 while.22
  26.0 0.6 add_compare_fusion.4
  27.5 1.8 %while.23 = (s32[]{:T(128)}, f32[128,8]{0,1:T(8,128)S(1)}, f32[128,8,128]{2,0,1:T(8,128)S(1)}, s32[]{:T(128)}, s32[]{:T(128)}, /*index=5*/bf16[128,8,128]{2,0,1:...) while((s32[]{:T(128)}, f32[128,8]{0,1:T(8,128)S(1)}, ...), condition=%wide.region_8.9_spmd, body=%wide.region_6.8_spmd.sunk | while | flops 271188992 | bytes 3691657 | solution.py:1105
  27.6 0.6 add_compare_fusion.5
  28.2 0.7 fusion.38
  29.4 0.9 copy_bitcast_fusion.heads_in
  30.3 0.7 copy-done.1
  31.0 98.1 %mix_blocks.1 = bf16[128,1024]{1,0:T(8,128)(2,1)} custom-call(bf16[128,1024]{1,0:T(8,128)(2,1)} %copy_bitcast_fusion.heads_in, bf16[128,1024]{1,0:T(8,128)(2,1)} %copy-done.1, bf16[1,4096]{1,0:T(2,128)(2,1)} %reshape.191.gain_ref, f32[512,1]{1,0:T(8,128)} %constant_dynamic-slice_fusion.gates_ref, bf16[1024,1024]{1,0:T(8,128)(2,1)} %outw_hbm.1, ...), custom_call_target="tpu_custom_call" | custom-call | tf_op jit(solution)/shard_map/mix_blocks/pallas_call | solution.py:988
  129.1 1.7 %copy.69 = bf16[128,1024]{1,0:T(8,128)(2,1)} copy(bf16[128,1024]{1,0:T(8,128)(2,1)} %mix_blocks.1) | data formatting | bytes 524288
  (48 shorter events, 3.6 us)
Async XLA Ops:
  0.6 14.9 %copy-start = (bf16[128,4096]{1,0:T(8,128)(2,1)S(1)}, bf16[128,4096]{1,0:T(8,128)(2,1)}, u32[]{:S(2)}) copy-start(bf16[128,4096]{1,0:T(8,128)(2,1)} %param.16) | copy-start | bytes 3145732
  0.6 15.6 %copy-start.2 = (bf16[128,1024]{1,0:T(8,128)(2,1)S(1)}, bf16[128,1024]{1,0:T(8,128)(2,1)}, u32[]{:S(2)}) copy-start(bf16[128,1024]{1,0:T(8,128)(2,1)} %param.17) | copy-start | bytes 786436
  0.7 15.8 %copy-start.3 = (bf16[128,2,256]{2,1,0:T(2,128)(2,1)S(1)}, bf16[128,2,256]{2,1,0:T(2,128)(2,1)}, u32[]{:S(2)}) copy-start(bf16[128,2,256]{2,1,0:T(2,128)(2,1)} %param.18) | copy-start | bytes 393220
  0.7 16.3 %copy-start.5 = (s32[4]{0:T(128)S(1)}, s32[4]{0:T(128)}, u32[]{:S(2)}) copy-start(s32[4]{0:T(128)} %param.21) | copy-start | bytes 52
  2.9 16.4 %collective-permute-start.3 = (f32[128,8]{0,1:T(8,128)S(1)}, f32[128,8]{0,1:T(8,128)S(1)}, u32[]{:S(2)}, u32[]{:S(2)}) collective-permute-start(f32[128,8]{0,1:T(8,128)S(1)} %select_reduce_fusion.1), channel_id=1, source_target_pairs={{0,12},{4,0},{8,4},{12,8},{1,13},{5,1},{9,5},{13,9},{2,14},{6,2},{... | collective-permute-start | bytes 12296 | tf_op jit(solution)/shard_map/ppermute | solution.py:1113
  5.3 13.9 %collective-permute-start.2 = (f32[128,8]{0,1:T(8,128)S(1)}, f32[128,8]{0,1:T(8,128)S(1)}, u32[]{:S(2)}, u32[]{:S(2)}) collective-permute-start(f32[128,8]{0,1:T(8,128)S(1)} %select_reduce_fusion.1), channel_id=1, source_target_pairs={{0,8},{4,12},{8,0},{12,4},{1,9},{5,13},{9,1},{13,5},{2,10},{6,14},... | collective-permute-start | bytes 12296 | tf_op jit(solution)/shard_map/ppermute | solution.py:1113
  5.9 13.3 %collective-permute-start.1 = (f32[128,8]{0,1:T(8,128)S(1)}, f32[128,8]{0,1:T(8,128)S(1)}, u32[]{:S(2)}, u32[]{:S(2)}) collective-permute-start(f32[128,8]{0,1:T(8,128)S(1)} %select_reduce_fusion.1), channel_id=1, source_target_pairs={{0,4},{4,8},{8,12},{12,0},{1,5},{5,9},{9,13},{13,1},{2,6},{6,10},{... | collective-permute-start | bytes 12296 | tf_op jit(solution)/shard_map/ppermute | solution.py:1113
  8.6 10.0 %copy-start.4 = (bf16[4096]{0:T(1024)(128)(2,1)S(1)}, bf16[4096]{0:T(1024)(128)(2,1)}, u32[]{:S(2)}) copy-start(bf16[4096]{0:T(1024)(128)(2,1)} %param.23) | copy-start | bytes 24580
  9.5 15.8 %all-to-all-start = ((bf16[16,32,256]{2,1,0:T(8,128)(2,1)}), bf16[16,32,256]{2,1,0:T(8,128)(2,1)S(1)}, u32[]{:S(2)}, u32[]{:S(2)}) async-start(bf16[16,32,256]{2,1,0:T(8,128)(2,1)} %broadcast_select_fusion), calls=%async_computation | async-start | bytes 524288 | tf_op jit(solution)/shard_map/all_to_all | solution.py:1049
  15.5 14.8 %collective-permute-start = (bf16[128,1024]{1,0:T(8,128)(2,1)S(1)}, bf16[128,1024]{1,0:T(8,128)(2,1)S(1)}, u32[]{:S(2)}, u32[]{:S(2)}) collective-permute-start(bf16[128,1024]{1,0:T(8,128)(2,1)S(1)} %constant_dynamic-slice_fusion.1), channel_id=1, source_target_pairs={{0,0},{1,4},{2,8},{3,12},{4,1},{5,5},{6,9},{7,13},{8,2},{9,6},{10,... | collective-permute-start | bytes 786440 | tf_op jit(solution)/shard_map/ppermute | solution.py:1130
  30.3 0.7 copy-start.1

commit v2 on v1

--- a/solution.py
+++ b/solution.py
@@ -10,7 +10,9 @@
 
 MESH = pl.DeviceIdType.MESH
 VMEM_BYTES = 60 * 1024 * 1024
-PIECE = 64
+PIECE = 32
+HOP = 3
+LAG = 3
 
 
 def place():
@@ -378,13 +380,17 @@
     donors,
     piece,
     heads_in,
-    hidden_ref,
     gain_ref,
-    gates_ref,
+    probs_ref,
+    ids_ref,
+    hidden_hbm,
     outw_hbm,
     raw_hbm,
     down_hbm,
     out_ref,
+    hidden_ref,
+    gates_out,
+    gates_in,
     outw_ref,
     raw_ref,
     down_ref,
@@ -400,6 +406,7 @@
     acc_ref,
     ssq_ref,
     act_ref,
+    gates_ref,
     part_ref,
     c_in,
     y_out,
@@ -410,6 +417,10 @@
     zl_in,
     local_sem,
     raw_sem,
+    g_send,
+    g_recv,
+    h_send,
+    h_recv,
     hy_send,
     hy_recv,
     hc_send,
@@ -438,14 +449,14 @@
     blocks, tokens, width = full_ref.shape
     model_width, ff_both = w_ref.shape
     ff_local = ff_both // 2
-    seqs_each = hidden_ref.shape[0] // suffix
+    seqs_each = hidden_ref.shape[0]
     per_seq = suffix // piece
     count = blocks * per_seq
     per_group = count // chips
     group_rows = 2 * suffix
     columns = out_ref.shape[1]
     last = donors - 1
-    lag = 2
+    lag = LAG
     first_mix = per_group + lag
     raw_steps, raw_slots, raw_rows = raw_sem.shape[0], raw_ref.shape[0], raw_ref.shape[1]
     relay = min(128, raw_rows)
@@ -470,9 +481,8 @@
     own_copies[2].start()
 
     barrier = pltpu.get_barrier_semaphore()
-    pl.semaphore_signal(barrier, inc=1, device_id={"expert": beside}, device_id_type=MESH)
-    for step in range(1, chips):
-        other = lax.rem(row + step, chips) * 2 + core
+    for step in range(1, blocks):
+        other = lax.rem(mine + step, blocks)
         pl.semaphore_signal(barrier, inc=1, device_id={"expert": other}, device_id_type=MESH)
 
     @pl.when(donor > 0)
@@ -485,7 +495,7 @@
 
     acc_ref[...] = jnp.zeros_like(acc_ref)
     ssq_ref[...] = jnp.zeros_like(ssq_ref)
-    pl.semaphore_wait(barrier, chips + jnp.minimum(donor, 1) + jnp.minimum(last - donor, 1))
+    pl.semaphore_wait(barrier, blocks - 1 + jnp.minimum(donor, 1) + jnp.minimum(last - donor, 1))
 
     def heads_of(seq):
         return heads_ref.at[pl.ds(pl.multiple_of(seq * suffix, suffix), suffix)]
@@ -495,11 +505,63 @@
 
     def heads_c(slot, seq):
         return send(heads_of(seq), heads_of(seq), hc_send, hc_recv, slot, expert=beside)
+
+    def gates_to(step):
+        return send(
+            gates_out.at[step],
+            gates_in.at[mine],
+            g_send,
+            g_recv,
+            step - 1,
+            expert=lax.rem(mine + step, blocks),
+        )
+
+    def partner(index):
+        return lax.rem(donor - lax.rem(mine, donors) + donors, donors) + donors * index
+
+    def hidden_to(index):
+        at = pl.ds(pl.multiple_of(partner(index) * width, width), width)
+        slot = mine // donors
+        return pltpu.make_async_remote_copy(
+            src_ref=hidden_hbm.at[:, at],
+            dst_ref=hidden_ref.at[slot],
+            send_sem=h_send.at[index],
+            recv_sem=h_recv.at[slot],
+            device_id={"expert": partner(index)},
+            device_id_type=MESH,
+        )
+
+    def hidden_own(index):
+        at = pl.ds(pl.multiple_of(mine * width, width), width)
+        return pltpu.make_async_copy(hidden_hbm.at[:, at], hidden_ref.at[index], h_recv.at[index])
 
     own_copies[1].wait()
     heads_c(0, mine).start()
     for step in range(1, chips):
         heads_y(step, mine, lax.rem(row + step, chips) * 2 + core).start()
+    for index in range(seqs_each):
+
+        @pl.when(partner(index) != mine)
+        def _():
+            hidden_to(index).start()
+
+        @pl.when(partner(index) == mine)
+        def _():
+            hidden_own(index).start()
+
+    square = (suffix, suffix)
+    eye = lax.broadcasted_iota(jnp.int32, square, 0) == lax.broadcasted_iota(jnp.int32, square, 1)
+    parts_of = donors // 2
+    share = probs_ref[...] / jnp.sum(probs_ref[...], axis=1, keepdims=True)
+    for step in range(blocks):
+        named = (lax.rem(mine + step, blocks) * donors + donor) // parts_of
+        column = jnp.sum(jnp.where(ids_ref[...] == named, share, 0.0), axis=1, keepdims=True)
+        line = jnp.sum(jnp.where(eye, column, 0.0), axis=0, keepdims=True)
+        if step:
+            gates_out[step] = jnp.broadcast_to(line, gates_out.shape[1:])
+            gates_to(step).start()
+        else:
+            gates_in[mine] = jnp.broadcast_to(line, gates_out.shape[1:])
     own_copies[0].wait()
 
     def seq_at(from_row, from_core, index):
@@ -524,7 +586,7 @@
         there = tile(from_row, from_core, chunk)
         return send(there, there, c_send, c_recv, step * count + chunk, expert=beside)
 
-    reach = jnp.maximum(donor, last - donor)
+    reach = jnp.maximum(donor, last - donor) * HOP
 
     def partial(index):
         seq = seq_at(row, core, index)
@@ -550,10 +612,12 @@
             preferred_element_type=jnp.float32,
         )
 
-        @pl.when(seq // seqs_each == donor)
-        def _():
-            top = pl.multiple_of(lax.rem(seq, seqs_each) * suffix, suffix)
-            p_ref[at, :] = p_ref[at, :] + hidden_ref[pl.ds(top, suffix), :].astype(jnp.float32)
+        for index in range(seqs_each):
+
+            @pl.when(partner(index) == seq)
+            def _():
+                hidden_own(index).wait()
+                p_ref[at, :] = p_ref[at, :] + hidden_ref[index].astype(jnp.float32)
 
     def p_rows(chunk):
         return p_ref[pl.ds(pl.multiple_of(chunk * piece, piece), piece), :]
@@ -632,7 +696,7 @@
         def _():
             partial(t // per_seq)
 
-        here = t - donor
+        here = t - donor * HOP
 
         @pl.when((here >= 0) & (here < count))
         def _():
@@ -652,7 +716,7 @@
             def _():
                 right(here).start()
 
-        there = t - (last - donor)
+        there = t - (last - donor) * HOP
 
         @pl.when((there >= 0) & (there < count))
         def _():
@@ -717,7 +781,7 @@
 
         return carry
 
-    steps = count + last + lag
+    steps = count + last * HOP + lag
     lax.fori_loop(0, steps, march, 0)
 
     def rest(index, carry):
@@ -727,14 +791,27 @@
     lax.fori_loop(jnp.minimum(steps - reach - first_mix, early), early, rest, 0)
     own_copies[2].wait()
 
+    for step in range(1, blocks):
+        back = lax.rem(mine + blocks - step, blocks)
+        send(
+            gates_out.at[step], gates_in.at[back], g_send, g_recv, step - 1, expert=back
+        ).wait_recv()
+
     def activate(group):
+        for side in range(2):
+            seq = group * 2 + side
+            gates_ref[side * suffix : (side + 1) * suffix, :] = jnp.sum(
+                jnp.where(eye, gates_in[seq][:1, :], 0.0), axis=1, keepdims=True
+            )
+
         def body(part, carry):
             at = pl.ds(pl.multiple_of(group * group_rows + part * strip, strip), strip)
+            here = pl.ds(pl.multiple_of(part * strip, strip), strip)
             mean = jnp.sum(ssq_ref[at, :], axis=1, keepdims=True) * (1.0 / model_width)
             inverse = lax.rsqrt(mean + 1e-06)
             gate = acc_ref[at, :ff_local] * inverse
             up = acc_ref[at, ff_local:] * inverse
-            value = gate / (1.0 + jnp.exp(-gate)) * up * gates_ref[at, :]
+            value = gate / (1.0 + jnp.exp(-gate)) * up * gates_ref[here, :]
             act_ref[at, :] = value.astype(act_ref.dtype)
             return carry
 
@@ -742,7 +819,7 @@
 
     def target(rank):
         low = jnp.minimum(donor, last - donor)
-        single = reach - low
+        single = jnp.maximum(donor, last - donor) - low
         rest_rank = rank - single
         gap = low - rest_rank // 2
         side = 1 - 2 * lax.rem(jnp.maximum(rest_rank, 0), 2)
@@ -897,6 +974,14 @@
 
     lax.fori_loop(0, donors, finish, 0)
 
+    for step in range(1, blocks):
+        gates_to(step).wait_send()
+    for index in range(seqs_each):
+
+        @pl.when(partner(index) != mine)
+        def _():
+            hidden_to(index).wait_send()
+
     for step in range(1, chips):
         heads_y(step, mine, mine).wait_send()
     for step in range(chips):
@@ -936,6 +1021,123 @@
         return carry
 
     lax.fori_loop(0, donors, drain_blocks, 0)
+
+
+def page_kernel(
+    experts,
+    donors,
+    pool_ref,
+    held_ref,
+    bias_ref,
+    query_ref,
+    fresh_ref,
+    head_ref,
+    out_buf,
+    pages_in,
+    sends,
+    recvs,
+):
+    expert, donor = lax.axis_index("expert"), lax.axis_index("donor")
+    seqs, kv_heads = out_buf.shape[0], out_buf.shape[1]
+    suffix, columns = head_ref.shape
+    head_dim = fresh_ref.shape[1] // 2
+    order = [
+        (step_e, step_z)
+        for step_z in [*far_first(donors), 0]
+        for step_e in range(experts)
+        if step_e or step_z
+    ]
+    barrier = pltpu.get_barrier_semaphore()
+
+    def ahead(step_e, step_z):
+        return lax.rem(expert + step_e, experts), lax.rem(donor + step_z, donors)
+
+    for step_e, step_z in order:
+        to_e, to_z = ahead(step_e, step_z)
+        pl.semaphore_signal(
+            barrier, inc=1, device_id={"expert": to_e, "donor": to_z}, device_id_type=MESH
+        )
+    for seq in range(seqs):
+        for group in range(kv_heads):
+            out_buf[seq, group] = pool_ref[held_ref[seq], group]
+    pl.semaphore_wait(barrier, experts * donors - 1)
+    mine = expert * donors + donor
+
+    def page(step_e, step_z):
+        to_e, to_z = ahead(step_e, step_z)
+        return send(
+            out_buf.at[to_e, to_z * kv_heads // donors],
+            pages_in.at[mine],
+            sends,
+            recvs,
+            step_e * donors + step_z,
+            expert=to_e,
+            donor=to_z,
+        )
+
+    for step_e, step_z in order:
+        page(step_e, step_z).start()
+    pages_in[mine] = out_buf[expert, donor * kv_heads // donors]
+    for step_e, step_z in order:
+        from_e, from_z = ahead(experts - step_e, donors - step_z)
+        send(
+            out_buf.at[expert, donor * kv_heads // donors],
+            pages_in.at[from_e * donors + from_z],
+            sends,
+            recvs,
+            step_e * donors + step_z,
+            expert=from_e,
+            donor=from_z,
+        ).wait_recv()
+    keys_count = pages_in.shape[0] * pages_in.shape[1]
+    causal = lax.broadcasted_iota(jnp.int32, (suffix, suffix), 0) >= lax.broadcasted_iota(
+        jnp.int32, (suffix, suffix), 1
+    )
+    scale = head_dim ** (-0.5)
+    both = (((1,), (1,)), ((), ()))
+    for left in range(0, columns, head_dim):
+        query = query_ref[:, left : left + head_dim]
+        old_keys = pages_in[:, :, :head_dim].reshape(keys_count, head_dim)
+        old = lax.dot_general(query, old_keys, both, preferred_element_type=jnp.float32)
+        new = lax.dot_general(
+            query, fresh_ref[:, :head_dim], both, preferred_element_type=jnp.float32
+        )
+        old = old * scale + bias_ref[...]
+        new = jnp.where(causal, new * scale, -jnp.inf)
+        top = jnp.maximum(
+            jnp.max(old, axis=1, keepdims=True), jnp.max(new, axis=1, keepdims=True)
+        )
+        old = jnp.exp(old - top)
+        new = jnp.exp(new - top)
+        total = jnp.sum(old, axis=1, keepdims=True) + jnp.sum(new, axis=1, keepdims=True)
+        old_vals = pages_in[:, :, head_dim:].reshape(keys_count, head_dim)
+        mixed = jnp.dot(old.astype(query.dtype), old_vals, preferred_element_type=jnp.float32)
+        mixed = mixed + jnp.dot(
+            new.astype(query.dtype), fresh_ref[:, head_dim:], preferred_element_type=jnp.float32
+        )
+        head_ref[:, left : left + head_dim] = (mixed / total).astype(head_ref.dtype)
+    for step_e, step_z in order:
+        page(step_e, step_z).wait_send()
+
+
+def page_heads(pool, held, bias, queries, fresh, experts, donors):
+    seqs, kv_heads, page_len, both = pool.shape
+    dma = pltpu.SemaphoreType.DMA
+    inside = pl.BlockSpec(memory_space=pltpu.VMEM)
+    return pl.pallas_call(
+        functools.partial(page_kernel, experts, donors),
+        out_shape=jax.ShapeDtypeStruct(queries.shape, queries.dtype),
+        in_specs=[inside, pl.BlockSpec(memory_space=pltpu.SMEM)] + [inside] * 3,
+        out_specs=inside,
+        scratch_shapes=[
+            pltpu.VMEM((seqs, kv_heads, page_len, both), pool.dtype),
+            pltpu.VMEM((experts * donors, page_len, both), pool.dtype),
+            dma((experts * donors,)),
+            dma((experts * donors,)),
+        ],
+        compiler_params=pltpu.CompilerParams(collective_id=4, has_side_effects=True),
+        name="page_heads",
+    )(pool, held, bias, queries, fresh)
 
 
 def mix_scratch(heads, out_weight, w_gate_up, chips, donors, piece):
@@ -951,6 +1153,9 @@
     wide = lambda *shape: pltpu.VMEM(shape, jnp.float32)
     held = lambda number: pltpu.VMEM((number, suffix, columns), kind)
     return [
+        vmem(blocks // donors, suffix, width),
+        wide(blocks, 8, suffix),
+        wide(blocks, 8, suffix),
         vmem(head_cols, width),
         vmem(3, model_width // 8, 2, ff_local),
         vmem(ff_local, model_width),
@@ -966,6 +1171,7 @@
         wide(tokens, 2 * ff_local),
         wide(tokens, 128),
         vmem(tokens, ff_local),
+        wide(2 * suffix, 1),
         vmem(chips * donors, 2 * suffix, columns),
         held(chips * donors),
         held((chips - 1) * donors),
@@ -977,7 +1183,9 @@
     ]
 
 
-def mix_blocks(heads, hidden, gain, gates, out_weight, w_gate_up, w_down, chips, donors, piece, scratch):
+def mix_blocks(
+    heads, gain, probs, ids, hidden, out_weight, w_gate_up, w_down, chips, donors, piece, scratch
+):
     suffix = heads.shape[0]
     columns = w_gate_up.shape[1] // donors
     count = 2 * chips * suffix // piece
@@ -988,10 +1196,12 @@
     return pl.pallas_call(
         functools.partial(mix_kernel, chips, donors, piece),
         out_shape=jax.ShapeDtypeStruct((suffix, columns), heads.dtype),
-        in_specs=[inside] * 4 + [outside] * 3,
+        in_specs=[inside] * 4 + [outside] * 4,
         out_specs=inside,
         scratch_shapes=scratch
         + [dma((3,)), dma((8,))]
+        + pair(2 * chips - 1)
+        + pair(2 * chips // donors)
         + pair(chips - 1)
         + pair(chips)
         + pair(count)
@@ -1006,7 +1216,7 @@
             collective_id=3, has_side_effects=True, vmem_limit_bytes=VMEM_BYTES
         ),
         name="mix_blocks",
-    )(heads, hidden, gain, gates, out_weight, w_gate_up, w_down)
+    )(heads, gain, probs, ids, hidden, out_weight, w_gate_up, w_down)
 
 
 def shards(
@@ -1041,6 +1251,35 @@
     owner_index = expert_index * n_donor + donor_index
     owner_of = page_table // seq_count
     held_slot = jnp.sum(jnp.where(owner_of == owner_index, page_table % seq_count, 0), axis=1)
+    chips = n_expert // 2
+    my_pair = lax.dynamic_index_in_dim(suffix_kv, my_group, 1, keepdims=False)
+    scratch = mix_scratch(queries, out_weight, w_gate_up, chips, n_donor, PIECE)
+    held_bytes = sum(math.prod(item.shape) * item.dtype.itemsize for item in scratch)
+    if held_bytes <= VMEM_BYTES - 4 * 1024 * 1024:
+        is_mine = (jnp.arange(seq_count) == expert_index)[:, None]
+        owned = owner_of[:, :, None] == jnp.arange(n_expert * n_donor)
+        place_of = jnp.arange(page_count)[None, :, None]
+        first = page_len * jnp.sum(jnp.where(owned & is_mine[:, :, None], place_of, 0), axis=(0, 1))
+        length = jnp.sum(jnp.where(is_mine[:, 0], prefix_len, 0))
+        seen = first[:, None] + jnp.arange(page_len) < length
+        bias = jnp.where(seen, 0.0, -jnp.inf).astype(jnp.float32).reshape(1, -1)
+        head_out = page_heads(kv_pool, held_slot, bias, queries, my_pair, n_expert, n_donor)
+        layer_out = mix_blocks(
+            head_out,
+            norm_gain.reshape(1, model_width),
+            route_probs,
+            expert_ids,
+            hidden_in,
+            out_weight,
+            w_gate_up,
+            w_down,
+            chips,
+            n_donor,
+            PIECE,
+            scratch,
+        )
+        return (layer_out, head_out)
+
     dest_group = jnp.arange(n_donor, dtype=jnp.int32) * kv_heads // n_donor
     wanted = (held_slot[:, None] * kv_heads + dest_group[None, :]).reshape(-1)
     outgoing = jnp.take(
@@ -1130,25 +1369,6 @@
         hidden_parts.append(lax.ppermute(sent, ("expert", "donor"), pairs))
     turned = lax.rem(expert_index - jnp.arange(seqs_each) + seqs_each * n_expert, seqs_each)
     hidden_block = jnp.stack(hidden_parts)[turned].reshape(seqs_each * suffix_len, width)
-
-    chips = n_expert // 2
-    scratch = mix_scratch(head_out, out_weight, w_gate_up, chips, n_donor, PIECE)
-    held_bytes = sum(math.prod(item.shape) * item.dtype.itemsize for item in scratch)
-    if held_bytes <= VMEM_BYTES - 4 * 1024 * 1024:
-        layer_out = mix_blocks(
-            head_out,
-            hidden_block,
-            norm_gain.reshape(1, model_width),
-            my_gates,
-            out_weight,
-            w_gate_up,
-            w_down,
-            chips,
-            n_donor,
-            PIECE,
-            scratch,
-        )
-        return (layer_out, head_out)
 
     heads_all = lax.all_gather(head_out, "expert", axis=0, tiled=True)
     w_in, heads_all = lax.optimization_barrier(

time: 131 us -> 115 us (0.88)
  starting transfers between devices: 9.91 us -> 0 us
  waiting for transfers between devices: 4.5 us -> 0 us
  Pallas kernels: 98.1 us -> 102 us
  other arithmetic: 6.36 us -> 3.49 us
  matrix products: 2.16 us -> 0 us
    pallas_call x0 -> x1, Pallas kernels: none -> 16.4 us  [page_heads(): pl.pallas_call(functools.partial(page_kernel, experts, donors), out_shape...]
    pallas_call x1, Pallas kernels: 98.1 us -> 86 us  [mix_blocks(): pl.pallas_call(functools.partial(mix_kernel, chips, donors, piece), out_s...]
    all_to_all x1 -> x0, starting transfers between devices: 6 us -> none  [shards(): lax.all_to_all(outgoing, ('expert', 'donor'), split_axis=0, concat_axis=0...]
    all_to_all x1 -> x0, waiting for transfers between devices: 4.49 us -> none  [shards(): lax.all_to_all(outgoing, ('expert', 'donor'), split_axis=0, concat_axis=0...]
    ppermute x4 -> x0, starting transfers between devices: 3.9 us -> none  [the longest x3 3.23 us: shards(): gate_tables.append(lax.ppermute(gate_table, 'expert', pairs))]
    unnamed x15 -> x9, local copies, waits for them, and re-layouts: 2.58 us -> 5.85 us
    gather x4 -> x0, local copies, waits for them, and re-layouts: 2.7 us -> none  [the longest x1 1.47 us: shards(): jnp.take(kv_pool.reshape(seq_count * kv_heads, page_len, 2 * head_dim), w...]
    dot_general x5 -> x0, matrix products: 2.16 us -> none  [the longest x2 1.22 us: block_scores(): jnp.einsum('thc,kc->thk', query_heads, keys_block, preferred_element_type...]
  transfers between devices with their start and end apart: 5 -> 0, of which waited for: 1 -> 0; matrix products, arithmetic and copies ran while one was open for 9% -> 0% of each run, Pallas kernels for 0% -> 0%
where the time goes in v2:
time: 115 us
  Pallas kernels  102 us (89%)
  local copies, waits for them, and re-layouts  7.94 us (7%)
  other arithmetic  3.49 us (3%)
    pallas_call x1, Pallas kernels, mix_blocks(): pl.pallas_call(functools.partial(mix_kernel, chips, donors, piece), out_s...  86 us
    pallas_call x1, Pallas kernels, page_heads(): pl.pallas_call(functools.partial(page_kernel, experts, donors), out_shape...  16.4 us
    unnamed x9, local copies, waits for them, and re-layouts  5.85 us

profile of v2, /device:TPU:0, one launch (start us, length us, event | category | flops | bytes accessed | tf_op | source)
XLA Modules:
  0.0 114.6 jit_solution(9531732798153676350)
XLA Ops:
  0.6 0.0 copy-start
  0.7 1.3 %select_reduce_fusion.1 = s32[]{:T(128)} fusion(s32[4]{0:T(128)} %param.17, s32[]{:T(128)S(6)} %axis_index.23), kind=kLoop, calls=%fused_computation.16 | loop fusion | flops 11 | bytes 24 | tf_op jit(solution)/shard_map/reduce_sum | solution.py:1263
  2.0 1.3 %fusion.3 = (s32[4]{0:T(128)}, s32[4,16]{1,0:T(4,128)S(1)}) fusion(s32[]{:T(128)S(6)} %add.36, s32[4,16]{1,0:T(4,128)} %param.16), kind=kLoop, calls=%fused_computation.12 | loop fusion | flops 1404 | bytes 532 | tf_op jit(solution)/shard_map/reduce_sum | solution.py:1253
  3.3 0.1 select_reduce_fusion
  3.4 0.7 fusion.1
  4.2 0.7 select_n.52.bias_ref
  4.8 1.3 %reshape.49.gain_ref = bf16[1,4096]{1,0:T(2,128)(2,1)} reshape(bf16[4096]{0:T(1024)(128)(2,1)} %param.19) | data formatting | bytes 16384 | tf_op jit(solution)/shard_map/reshape | solution.py:1269
  6.1 1.4 %copy.21.ids_ref = s32[128,4]{1,0:T(8,128)} copy(s32[128,4]{0,1:T(4,128)} %param.20) | data formatting | bytes 4096 | tf_op args[8]
  7.5 1.4 %copy.20.probs_ref = f32[128,4]{1,0:T(8,128)} copy(f32[128,4]{0,1:T(4,128)} %param.21) | data formatting | bytes 4096 | tf_op args[9]
  8.9 0.0 copy-done
  8.9 0.1 constant_dynamic-slice_fusion
  9.1 0.6 copy.24
  9.7 16.4 %page_heads.1.heads_in = bf16[128,1024]{1,0:T(8,128)(2,1)} custom-call(bf16[4,2,32,256]{3,2,1,0:T(8,128)(2,1)} %pool_ref.1, s32[4]{0:T(128)} %get-tuple-element.2.held_ref, f32[1,512]{1,0:T(1,128)} %select_n.52.bias_ref, bf16[128,1024]{1,0:T(8,128)(2,1)} %query_ref.1, bf16[128,256]{1,0:T(8,128)(2,1)} %bitcast.3), custom_call_target="tpu_custom_call" | custom-call | tf_op jit(solution)/shard_map/page_heads/pallas_call | solution.py:1127
  26.1 0.0 copy-start.1
  26.1 86.0 %mix_blocks.1 = bf16[128,1024]{1,0:T(8,128)(2,1)} custom-call(bf16[128,1024]{1,0:T(8,128)(2,1)} %page_heads.1.heads_in, bf16[1,4096]{1,0:T(2,128)(2,1)} %reshape.49.gain_ref, f32[128,4]{1,0:T(8,128)} %copy.20.probs_ref, s32[128,4]{1,0:T(8,128)} %copy.21.ids_ref, bf16[128,4096]{1,0:T(8,128)(2,1)} %hidden_hbm.1, bf16[1024,1024]{1,0:T(8,128)(2,1)} %outw_hbm.1, ...), custom_call_target="tpu_custom_call" | custom-call | tf_op jit(solution)/shard_map/mix_blocks/pallas_call | solution.py:1196
  112.2 1.7 %copy.27 = bf16[128,1024]{1,0:T(8,128)(2,1)} copy(bf16[128,1024]{1,0:T(8,128)(2,1)} %mix_blocks.1) | data formatting | bytes 524288
  113.9 0.0 copy-done.1
  113.9 0.7 copy.28
  (2 shorter events, 0.0 us)
Async XLA Ops:
  0.6 8.3 %copy-start = (bf16[128,2,256]{2,1,0:T(2,128)(2,1)S(1)}, bf16[128,2,256]{2,1,0:T(2,128)(2,1)}, u32[]{:S(2)}) copy-start(bf16[128,2,256]{2,1,0:T(2,128)(2,1)} %param.14) | copy-start | bytes 393220
  26.1 87.7 %copy-start.1 = (bf16[128,1024]{1,0:T(8,128)(2,1)S(1)}, bf16[128,1024]{1,0:T(8,128)(2,1)}, u32[]{:S(2)}) copy-start(bf16[128,1024]{1,0:T(8,128)(2,1)} %page_heads.1.heads_in) | copy-start | bytes 786436

commit v3 on v2

--- a/solution.py
+++ b/solution.py
@@ -391,6 +391,7 @@
     hidden_ref,
     gates_out,
     gates_in,
+    gain_wide,
     outw_ref,
     raw_ref,
     down_ref,
@@ -493,6 +494,7 @@
     def _():
         pl.semaphore_signal(barrier, inc=1, device_id={"donor": donor + 1}, device_id_type=MESH)
 
+    gain_wide[...] = gain_ref[...].astype(jnp.float32)
     acc_ref[...] = jnp.zeros_like(acc_ref)
     ssq_ref[...] = jnp.zeros_like(ssq_ref)
     pl.semaphore_wait(barrier, blocks - 1 + jnp.minimum(donor, 1) + jnp.minimum(last - donor, 1))
@@ -552,11 +554,10 @@
     square = (suffix, suffix)
     eye = lax.broadcasted_iota(jnp.int32, square, 0) == lax.broadcasted_iota(jnp.int32, square, 1)
     parts_of = donors // 2
-    share = probs_ref[...] / jnp.sum(probs_ref[...], axis=1, keepdims=True)
+    share = probs_ref[...] / jnp.sum(probs_ref[...], axis=0, keepdims=True)
     for step in range(blocks):
         named = (lax.rem(mine + step, blocks) * donors + donor) // parts_of
-        column = jnp.sum(jnp.where(ids_ref[...] == named, share, 0.0), axis=1, keepdims=True)
-        line = jnp.sum(jnp.where(eye, column, 0.0), axis=0, keepdims=True)
+        line = jnp.sum(jnp.where(ids_ref[...] == named, share, 0.0), axis=0, keepdims=True)
         if step:
             gates_out[step] = jnp.broadcast_to(line, gates_out.shape[1:])
             gates_to(step).start()
@@ -663,18 +664,20 @@
         group = lax.rem(from_row + turn, chips)
         top = pl.multiple_of(group * group_rows, group_rows)
         left_at = pl.multiple_of(block * width, width)
-        gain = gain_ref[:, pl.ds(left_at, width)].astype(jnp.float32)
+        lanes = gain_wide.shape[1]
+        tiles = width // lanes
+        gain = gain_wide[pl.ds(pl.multiple_of(block * tiles, tiles), tiles), :]
 
         def scale(part, carry):
             here = pl.ds(pl.multiple_of(part * strip, strip), strip)
             at = pl.ds(pl.multiple_of(top + part * strip, strip), strip)
-            value = full_ref[block, at, :].astype(jnp.float32)
-            x_ref[here, :] = (value * gain).astype(x_ref.dtype)
-            square = value * value
-            total = square[:, :128]
-            for start in range(128, width, 128):
-                total = total + square[:, start : start + 128]
-            ssq_ref[at, :] = ssq_ref[at, :] + total
+            total = ssq_ref[at, :]
+            for part_at in range(tiles):
+                wide = slice(part_at * lanes, (part_at + 1) * lanes)
+                value = full_ref[block, at, wide].astype(jnp.float32)
+                x_ref[here, wide] = (value * gain[part_at : part_at + 1, :]).astype(x_ref.dtype)
+                total = total + value * value
+            ssq_ref[at, :] = total
             return carry
 
         lax.fori_loop(0, group_rows // strip, scale, 0)
@@ -1027,8 +1030,8 @@
     experts,
     donors,
     pool_ref,
-    held_ref,
-    bias_ref,
+    table_ref,
+    length_ref,
     query_ref,
     fresh_ref,
     head_ref,
@@ -1057,11 +1060,24 @@
         pl.semaphore_signal(
             barrier, inc=1, device_id={"expert": to_e, "donor": to_z}, device_id_type=MESH
         )
+    mine = expert * donors + donor
+    pages, page_len = table_ref.shape[1], pages_in.shape[1]
+    slots = seqs
     for seq in range(seqs):
+        held = 0
+        for index in range(pages):
+            named = table_ref[seq, index]
+            held = held + jnp.where(named // slots == mine, named % slots, 0)
         for group in range(kv_heads):
-            out_buf[seq, group] = pool_ref[held_ref[seq], group]
+            out_buf[seq, group] = pool_ref[held, group]
+    lane = lax.broadcasted_iota(jnp.int32, (1, pages * page_len), 1)
+    holder = lane // page_len
+    first = jnp.zeros_like(lane)
+    for index in range(pages):
+        first = jnp.where(holder == table_ref[expert, index] // slots, index * page_len, first)
+    seen = first + lane % page_len < length_ref[expert]
+    bias = jnp.where(seen, 0.0, -jnp.inf)
     pl.semaphore_wait(barrier, experts * donors - 1)
-    mine = expert * donors + donor
 
     def page(step_e, step_z):
         to_e, to_z = ahead(step_e, step_z)
@@ -1102,7 +1118,7 @@
         new = lax.dot_general(
             query, fresh_ref[:, :head_dim], both, preferred_element_type=jnp.float32
         )
-        old = old * scale + bias_ref[...]
+        old = old * scale + bias
         new = jnp.where(causal, new * scale, -jnp.inf)
         top = jnp.maximum(
             jnp.max(old, axis=1, keepdims=True), jnp.max(new, axis=1, keepdims=True)
@@ -1120,14 +1136,14 @@
         page(step_e, step_z).wait_send()
 
 
-def page_heads(pool, held, bias, queries, fresh, experts, donors):
+def page_heads(pool, table, lengths, queries, fresh, experts, donors):
     seqs, kv_heads, page_len, both = pool.shape
     dma = pltpu.SemaphoreType.DMA
     inside = pl.BlockSpec(memory_space=pltpu.VMEM)
     return pl.pallas_call(
         functools.partial(page_kernel, experts, donors),
         out_shape=jax.ShapeDtypeStruct(queries.shape, queries.dtype),
-        in_specs=[inside, pl.BlockSpec(memory_space=pltpu.SMEM)] + [inside] * 3,
+        in_specs=[inside] + [pl.BlockSpec(memory_space=pltpu.SMEM)] * 2 + [inside] * 2,
         out_specs=inside,
         scratch_shapes=[
             pltpu.VMEM((seqs, kv_heads, page_len, both), pool.dtype),
@@ -1137,7 +1153,7 @@
         ],
         compiler_params=pltpu.CompilerParams(collective_id=4, has_side_effects=True),
         name="page_heads",
-    )(pool, held, bias, queries, fresh)
+    )(pool, table, lengths, queries, fresh)
 
 
 def mix_scratch(heads, out_weight, w_gate_up, chips, donors, piece):
@@ -1156,6 +1172,7 @@
         vmem(blocks // donors, suffix, width),
         wide(blocks, 8, suffix),
         wide(blocks, 8, suffix),
+        wide(model_width // 128, 128),
         vmem(head_cols, width),
         vmem(3, model_width // 8, 2, ff_local),
         vmem(ff_local, model_width),
@@ -1256,19 +1273,14 @@
     scratch = mix_scratch(queries, out_weight, w_gate_up, chips, n_donor, PIECE)
     held_bytes = sum(math.prod(item.shape) * item.dtype.itemsize for item in scratch)
     if held_bytes <= VMEM_BYTES - 4 * 1024 * 1024:
-        is_mine = (jnp.arange(seq_count) == expert_index)[:, None]
-        owned = owner_of[:, :, None] == jnp.arange(n_expert * n_donor)
-        place_of = jnp.arange(page_count)[None, :, None]
-        first = page_len * jnp.sum(jnp.where(owned & is_mine[:, :, None], place_of, 0), axis=(0, 1))
-        length = jnp.sum(jnp.where(is_mine[:, 0], prefix_len, 0))
-        seen = first[:, None] + jnp.arange(page_len) < length
-        bias = jnp.where(seen, 0.0, -jnp.inf).astype(jnp.float32).reshape(1, -1)
-        head_out = page_heads(kv_pool, held_slot, bias, queries, my_pair, n_expert, n_donor)
+        head_out = page_heads(
+            kv_pool, page_table, prefix_len, queries, my_pair, n_expert, n_donor
+        )
         layer_out = mix_blocks(
             head_out,
-            norm_gain.reshape(1, model_width),
-            route_probs,
-            expert_ids,
+            norm_gain.reshape(-1, 128),
+            route_probs.T,
+            expert_ids.T,
             hidden_in,
             out_weight,
             w_gate_up,

time: 115 us -> 107 us (0.930)
  local copies, waits for them, and re-layouts: 7.94 us -> 4.04 us
  other arithmetic: 3.49 us -> 0 us
    reduce_sum x3 -> x0, other arithmetic: 2.76 us -> none  [the longest x1 1.34 us: shards(): jnp.sum(jnp.where(owner_of == owner_index, page_table % seq_count, 0), ax...]
    unnamed x9 -> x7, local copies, waits for them, and re-layouts: 5.85 us -> 3.9 us
    reshape x1 -> x0, local copies, waits for them, and re-layouts: 1.3 us -> none  [shards(): norm_gain.reshape(1, model_width)]
where the time goes in v3:
time: 107 us
  Pallas kernels  102 us (95%)
  local copies, waits for them, and re-layouts  4.04 us (4%)
    pallas_call x1, Pallas kernels, mix_blocks(): pl.pallas_call(functools.partial(mix_kernel, chips, donors, piece), out_s...  85.8 us
    pallas_call x1, Pallas kernels, page_heads(): pl.pallas_call(functools.partial(page_kernel, experts, donors), out_shape...  16.4 us
    unnamed x7, local copies, waits for them, and re-layouts  3.9 us

profile of v3, /device:TPU:0, one launch (start us, length us, event | category | flops | bytes accessed | tf_op | source)
XLA Modules:
  0.0 106.9 jit_solution(1452249822350207494)
XLA Ops:
  0.6 0.0 copy-start
  0.7 0.9 copy-done
  1.5 0.1 constant_dynamic-slice_fusion
  1.7 0.6 copy.17
  2.3 16.4 %page_heads.1.heads_in = bf16[128,1024]{1,0:T(8,128)(2,1)} custom-call(bf16[4,2,32,256]{3,2,1,0:T(8,128)(2,1)} %pool_ref.1, s32[4,16]{1,0:T(4,128)} %table_ref.1, s32[4]{0:T(128)} %length_ref.1, bf16[128,1024]{1,0:T(8,128)(2,1)} %query_ref.1, bf16[128,256]{1,0:T(8,128)(2,1)} %bitcast.6), custom_call_target="tpu_custom_call" | custom-call | tf_op jit(solution)/shard_map/page_heads/pallas_call | solution.py:1143
  18.7 0.0 copy-start.1
  18.7 85.8 %mix_blocks.1 = bf16[128,1024]{1,0:T(8,128)(2,1)} custom-call(bf16[128,1024]{1,0:T(8,128)(2,1)} %page_heads.1.heads_in, bf16[32,128]{1,0:T(8,128)(2,1)} %bitcast.7, f32[4,128]{1,0:T(4,128)} %bitcast.8, s32[4,128]{1,0:T(4,128)} %bitcast.9, bf16[128,4096]{1,0:T(8,128)(2,1)} %hidden_hbm.1, bf16[1024,1024]{1,0:T(8,128)(2,1)} %outw_hbm.1, ...), custom_call_target="tpu_custom_call" | custom-call | tf_op jit(solution)/shard_map/mix_blocks/pallas_call | solution.py:1213
  104.5 1.7 %copy.20 = bf16[128,1024]{1,0:T(8,128)(2,1)} copy(bf16[128,1024]{1,0:T(8,128)(2,1)} %mix_blocks.1) | data formatting | bytes 524288
  106.2 0.0 copy-done.1
  106.2 0.7 copy.21
Async XLA Ops:
  0.6 0.9 copy-start
  18.7 87.5 %copy-start.1 = (bf16[128,1024]{1,0:T(8,128)(2,1)S(1)}, bf16[128,1024]{1,0:T(8,128)(2,1)}, u32[]{:S(2)}) copy-start(bf16[128,1024]{1,0:T(8,128)(2,1)} %page_heads.1.heads_in) | copy-start | bytes 786436

commit v4 on v3

--- a/solution.py
+++ b/solution.py
@@ -453,12 +453,12 @@
     seqs_each = hidden_ref.shape[0]
     per_seq = suffix // piece
     count = blocks * per_seq
-    per_group = count // chips
-    group_rows = 2 * suffix
+    half, half_count, per_half = suffix // 2, count // 2, per_seq // 2
+    rows = blocks * half
     columns = out_ref.shape[1]
     last = donors - 1
     lag = LAG
-    first_mix = per_group + lag
+    first_mix = half_count + lag
     raw_steps, raw_slots, raw_rows = raw_sem.shape[0], raw_ref.shape[0], raw_ref.shape[1]
     relay = min(128, raw_rows)
     strip = 16
@@ -568,9 +568,15 @@
     def seq_at(from_row, from_core, index):
         return lax.rem(from_row + index // 2, chips) * 2 + lax.rem(from_core + lax.rem(index, 2), 2)
 
+    def spot(chunk):
+        within = lax.rem(chunk, half_count)
+        offset = chunk // half_count * half + lax.rem(within, per_half) * piece
+        return within // per_half, offset
+
     def tile(from_row, from_core, chunk):
-        seq = seq_at(from_row, from_core, chunk // per_seq)
-        top = pl.multiple_of(seq * suffix + lax.rem(chunk, per_seq) * piece, piece)
+        index, offset = spot(chunk)
+        seq = seq_at(from_row, from_core, index)
+        top = pl.multiple_of(seq * suffix + offset, piece)
         return full_ref.at[from_row * 2 + from_core, pl.ds(top, piece)]
 
     def right(chunk):
@@ -621,7 +627,8 @@
                 p_ref[at, :] = p_ref[at, :] + hidden_ref[index].astype(jnp.float32)
 
     def p_rows(chunk):
-        return p_ref[pl.ds(pl.multiple_of(chunk * piece, piece), piece), :]
+        index, offset = spot(chunk)
+        return p_ref[pl.ds(pl.multiple_of(index * suffix + offset, piece), piece), :]
 
     def relay_weights(index):
         raw_copy(index).wait()
@@ -655,14 +662,13 @@
         @pl.when(lax.rem(index, 2) == 1)
         def _():
             def body(chunk, carry):
-                over(back, turn * per_group + chunk, from_row, from_core).wait_recv()
+                over(back, turn * half_count + chunk, from_row, from_core).wait_recv()
                 return carry
 
-            lax.fori_loop(0, per_group, body, 0)
+            lax.fori_loop(0, half_count, body, 0)
 
         block = from_row * 2 + from_core
-        group = lax.rem(from_row + turn, chips)
-        top = pl.multiple_of(group * group_rows, group_rows)
+        top = pl.multiple_of(turn * rows, rows)
         left_at = pl.multiple_of(block * width, width)
         lanes = gain_wide.shape[1]
         tiles = width // lanes
@@ -671,17 +677,21 @@
         def scale(part, carry):
             here = pl.ds(pl.multiple_of(part * strip, strip), strip)
             at = pl.ds(pl.multiple_of(top + part * strip, strip), strip)
+            seq, inside = part * strip // half, lax.rem(part * strip, half)
+            source = pl.ds(
+                pl.multiple_of(seq * suffix + turn * half + inside, strip), strip
+            )
             total = ssq_ref[at, :]
             for part_at in range(tiles):
                 wide = slice(part_at * lanes, (part_at + 1) * lanes)
-                value = full_ref[block, at, wide].astype(jnp.float32)
+                value = full_ref[block, source, wide].astype(jnp.float32)
                 x_ref[here, wide] = (value * gain[part_at : part_at + 1, :]).astype(x_ref.dtype)
                 total = total + value * value
             ssq_ref[at, :] = total
             return carry
 
-        lax.fori_loop(0, group_rows // strip, scale, 0)
-        at = pl.ds(top, group_rows)
+        lax.fori_loop(0, rows // strip, scale, 0)
+        at = pl.ds(top, rows)
 
         def multiply(part, carry):
             wide = pl.ds(pl.multiple_of(part * cut, cut), cut)
@@ -692,133 +702,30 @@
 
         lax.fori_loop(0, ff_both // cut, multiply, 0)
 
-    early = blocks * (chips - 1)
-
-    def march(t, carry):
-        @pl.when((t < count) & (lax.rem(t, per_seq) == 0))
-        def _():
-            partial(t // per_seq)
-
-        here = t - donor * HOP
-
-        @pl.when((here >= 0) & (here < count))
-        def _():
-            @pl.when(donor == 0)
-            def _():
-                r_out[here] = p_rows(here).astype(r_out.dtype)
-
-            @pl.when(donor > 0)
-            def _():
-                right(here).wait_recv()
-
-            @pl.when((donor > 0) & (donor < last))
-            def _():
-                r_out[here] = (p_rows(here) + r_in[here].astype(jnp.float32)).astype(r_out.dtype)
-
-            @pl.when(donor < last)
-            def _():
-                right(here).start()
-
-        there = t - (last - donor) * HOP
-
-        @pl.when((there >= 0) & (there < count))
-        def _():
-            @pl.when(donor == last)
-            def _():
-                l_out[there] = p_rows(there).astype(l_out.dtype)
-
-            @pl.when(donor < last)
-            def _():
-                left(there).wait_recv()
-
-            @pl.when((donor > 0) & (donor < last))
-            def _():
-                l_out[there] = (p_rows(there) + l_in[there].astype(jnp.float32)).astype(l_out.dtype)
-
-            @pl.when(donor > 0)
-            def _():
-                left(there).start()
-
-        done = t - reach
-
-        @pl.when((done >= 0) & (done < count))
-        def _():
-            goal = tile(row, core, done)
-
-            @pl.when(donor == 0)
-            def _():
-                goal[...] = (p_rows(done) + l_in[done].astype(jnp.float32)).astype(goal.dtype)
-
-            @pl.when(donor == last)
-            def _():
-                goal[...] = (p_rows(done) + r_in[done].astype(jnp.float32)).astype(goal.dtype)
-
-            @pl.when((donor > 0) & (donor < last))
-            def _():
-                goal[...] = (
-                    p_rows(done) + r_in[done].astype(jnp.float32) + l_in[done].astype(jnp.float32)
-                ).astype(goal.dtype)
-
-            for step in range(1, chips):
-                across(step, done, row, lax.rem(row + step, chips) * 2 + core).start()
-            over(0, done, row, core).start()
-
-        came = t - reach - lag
-
-        @pl.when((came >= 0) & (came < count))
-        def _():
-            for step in range(1, chips):
-                from_row = lax.rem(row + chips - step, chips)
-                across(step, came, from_row, from_row * 2 + core).wait_recv()
-                over(step, came, from_row, core).start()
-
-        @pl.when(t < raw_steps)
-        def _():
-            relay_weights(t)
-
-        ready = t - reach - first_mix
-
-        @pl.when((ready >= 0) & (ready < early))
-        def _():
-            mix(ready // blocks, lax.rem(ready, blocks))
-
-        return carry
-
-    steps = count + last * HOP + lag
-    lax.fori_loop(0, steps, march, 0)
-
-    def rest(index, carry):
-        mix(index // blocks, lax.rem(index, blocks))
-        return carry
-
-    lax.fori_loop(jnp.minimum(steps - reach - first_mix, early), early, rest, 0)
-    own_copies[2].wait()
-
-    for step in range(1, blocks):
-        back = lax.rem(mine + blocks - step, blocks)
-        send(
-            gates_out.at[step], gates_in.at[back], g_send, g_recv, step - 1, expert=back
-        ).wait_recv()
-
-    def activate(group):
-        for side in range(2):
-            seq = group * 2 + side
-            gates_ref[side * suffix : (side + 1) * suffix, :] = jnp.sum(
-                jnp.where(eye, gates_in[seq][:1, :], 0.0), axis=1, keepdims=True
-            )
-
+    def weigh():
+        for step in range(1, blocks):
+            back = lax.rem(mine + blocks - step, blocks)
+            send(
+                gates_out.at[step], gates_in.at[back], g_send, g_recv, step - 1, expert=back
+            ).wait_recv()
+        for seq in range(blocks):
+            column = jnp.sum(jnp.where(eye, gates_in[seq][:1, :], 0.0), axis=1, keepdims=True)
+            for turn in range(2):
+                top = turn * rows + seq * half
+                gates_ref[top : top + half, :] = column[turn * half : (turn + 1) * half, :]
+
+    def activate(turn):
         def body(part, carry):
-            at = pl.ds(pl.multiple_of(group * group_rows + part * strip, strip), strip)
-            here = pl.ds(pl.multiple_of(part * strip, strip), strip)
+            at = pl.ds(pl.multiple_of(turn * rows + part * strip, strip), strip)
             mean = jnp.sum(ssq_ref[at, :], axis=1, keepdims=True) * (1.0 / model_width)
             inverse = lax.rsqrt(mean + 1e-06)
             gate = acc_ref[at, :ff_local] * inverse
             up = acc_ref[at, ff_local:] * inverse
-            value = gate / (1.0 + jnp.exp(-gate)) * up * gates_ref[here, :]
+            value = gate / (1.0 + jnp.exp(-gate)) * up * gates_ref[at, :]
             act_ref[at, :] = value.astype(act_ref.dtype)
             return carry
 
-        lax.fori_loop(0, group_rows // strip, body, 0)
+        lax.fori_loop(0, rows // strip, body, 0)
 
     def target(rank):
         low = jnp.minimum(donor, last - donor)
@@ -839,109 +746,223 @@
             out[at, :] = value.astype(out.dtype)
             return carry
 
-        lax.fori_loop(0, suffix // strip, body, 0)
+        lax.fori_loop(0, half // strip, body, 0)
 
     order = list(range(1, chips)) + [0]
 
-    def own_half(slot):
-        return part_ref.at[slot, pl.ds(pl.multiple_of(core * suffix, suffix), suffix)]
-
-    def swap(slot):
-        away = part_ref.at[slot, pl.ds(pl.multiple_of((1 - core) * suffix, suffix), suffix)]
-        return send(away, c_in.at[slot], cc_send, cc_recv, slot, expert=beside)
+    def own_rows(slot, to_row):
+        top = pl.multiple_of((to_row * 2 + core) * half, half)
+        return part_ref.at[slot, pl.ds(top, half)]
+
+    def swap(slot, to_row):
+        top = pl.multiple_of((to_row * 2 + 1 - core) * half, half)
+        place_in = slot * chips + to_row
+        return send(
+            part_ref.at[slot, pl.ds(top, half)],
+            c_in.at[place_in],
+            cc_send,
+            cc_recv,
+            place_in,
+            expert=beside,
+        )
 
     def cross(hop, to):
         return send(y_out.at[hop], y_in.at[hop], yy_send, yy_recv, hop, expert=to)
 
-    def produce(step, rank):
-        slot = step * donors + rank
-        top = pl.multiple_of(lax.rem(row + step, chips) * group_rows, group_rows)
-        left_at = pl.multiple_of(target(rank) * columns, columns)
+    def produce(slot):
+        top = pl.multiple_of(slot // donors * rows, rows)
+        left_at = pl.multiple_of(target(lax.rem(slot, donors)) * columns, columns)
         part_ref[slot] = jnp.dot(
-            act_ref[pl.ds(top, group_rows), :],
+            act_ref[pl.ds(top, rows), :],
             down_ref[:, pl.ds(left_at, columns)],
             preferred_element_type=jnp.float32,
         ).astype(part_ref.dtype)
-        swap(slot).start()
-
-    def pass_on(step, rank):
-        slot = step * donors + rank
-        hop = (step - 1) * donors + rank
-        swap(slot).wait_recv()
-        add(y_out.at[hop], own_half(slot), c_in.at[slot])
-        cross(hop, lax.rem(row + step, chips) * 2 + core).start()
-
-    for step in order:
-        for side in range(2):
-            mix(chips - 1, 2 * ((step + 1) % chips) + side)
-        activate(lax.rem(row + step, chips))
-        if step:
-
-            def body(rank, carry):
-                produce(step, rank)
-
-                @pl.when(rank > 0)
-                def _():
-                    pass_on(step, rank - 1)
-
-                return carry
-
-            lax.fori_loop(0, donors, body, 0)
-            pass_on(step, donors - 1)
-        else:
-
-            def body(rank, carry):
-                produce(0, rank)
-                return carry
-
-            lax.fori_loop(0, donors, body, 0)
-
-    def shift_right(goal):
-        return send(zr_out.at[goal], zr_in.at[goal], zr_send, zr_recv, goal, donor=donor + 1)
-
-    def shift_left(goal):
-        return send(zl_out.at[goal], zl_in.at[goal], zl_send, zl_recv, goal, donor=donor - 1)
-
-    def finish(rank, carry):
-        goal = target(rank)
-        swap(rank).wait_recv()
-        terms = [own_half(rank), c_in.at[rank]]
+        for step in order:
+            swap(slot, lax.rem(row + step, chips)).start()
+
+    def pass_on(slot):
         for step in range(1, chips):
-            hop = (step - 1) * donors + rank
+            to_row = lax.rem(row + step, chips)
+            hop = (step - 1) * 2 * donors + slot
+            swap(slot, to_row).wait_recv()
+            add(y_out.at[hop], own_rows(slot, to_row), c_in.at[slot * chips + to_row])
+            cross(hop, to_row * 2 + core).start()
+
+    stages = blocks + 1 + donors + 1
+
+    def task(index):
+        turn, stage = index // stages, lax.rem(index, stages)
+
+        @pl.when(stage < blocks)
+        def _():
+            mix(turn, stage)
+
+        @pl.when(stage == blocks)
+        def _():
+            @pl.when(turn == 0)
+            def _():
+                own_copies[2].wait()
+                weigh()
+
+            activate(turn)
+
+        slot = turn * donors + stage - blocks - 1
+
+        @pl.when((stage > blocks) & (stage < stages - 1))
+        def _():
+            produce(slot)
+
+        @pl.when(stage > blocks + 1)
+        def _():
+            pass_on(slot - 1)
+
+    def march(t, carry):
+        @pl.when((t < half_count) & (lax.rem(t, per_half) == 0))
+        def _():
+            partial(t // per_half)
+
+        here = t - donor * HOP
+
+        @pl.when((here >= 0) & (here < count))
+        def _():
+            @pl.when(donor == 0)
+            def _():
+                r_out[here] = p_rows(here).astype(r_out.dtype)
+
+            @pl.when(donor > 0)
+            def _():
+                right(here).wait_recv()
+
+            @pl.when((donor > 0) & (donor < last))
+            def _():
+                r_out[here] = (p_rows(here) + r_in[here].astype(jnp.float32)).astype(r_out.dtype)
+
+            @pl.when(donor < last)
+            def _():
+                right(here).start()
+
+        there = t - (last - donor) * HOP
+
+        @pl.when((there >= 0) & (there < count))
+        def _():
+            @pl.when(donor == last)
+            def _():
+                l_out[there] = p_rows(there).astype(l_out.dtype)
+
+            @pl.when(donor < last)
+            def _():
+                left(there).wait_recv()
+
+            @pl.when((donor > 0) & (donor < last))
+            def _():
+                l_out[there] = (p_rows(there) + l_in[there].astype(jnp.float32)).astype(l_out.dtype)
+
+            @pl.when(donor > 0)
+            def _():
+                left(there).start()
+
+        done = t - reach
+
+        @pl.when((done >= 0) & (done < count))
+        def _():
+            goal = tile(row, core, done)
+
+            @pl.when(donor == 0)
+            def _():
+                goal[...] = (p_rows(done) + l_in[done].astype(jnp.float32)).astype(goal.dtype)
+
+            @pl.when(donor == last)
+            def _():
+                goal[...] = (p_rows(done) + r_in[done].astype(jnp.float32)).astype(goal.dtype)
+
+            @pl.when((donor > 0) & (donor < last))
+            def _():
+                goal[...] = (
+                    p_rows(done) + r_in[done].astype(jnp.float32) + l_in[done].astype(jnp.float32)
+                ).astype(goal.dtype)
+
+            for step in range(1, chips):
+                across(step, done, row, lax.rem(row + step, chips) * 2 + core).start()
+            over(0, done, row, core).start()
+
+        came = t - reach - lag
+
+        @pl.when((came >= 0) & (came < count))
+        def _():
+            for step in range(1, chips):
+                from_row = lax.rem(row + chips - step, chips)
+                across(step, came, from_row, from_row * 2 + core).wait_recv()
+                over(step, came, from_row, core).start()
+
+        @pl.when(t < raw_steps)
+        def _():
+            relay_weights(t)
+
+        ready = t - reach - first_mix
+
+        @pl.when((ready >= 0) & (ready < stages))
+        def _():
+            task(ready)
+
+        return carry
+
+    steps = count + last * HOP + lag
+    lax.fori_loop(0, steps, march, 0)
+
+    def rest(index, carry):
+        task(index)
+        return carry
+
+    lax.fori_loop(jnp.minimum(steps - reach - first_mix, stages), 2 * stages, rest, 0)
+
+    def shift_right(key):
+        return send(zr_out.at[key], zr_in.at[key], zr_send, zr_recv, key, donor=donor + 1)
+
+    def shift_left(key):
+        return send(zl_out.at[key], zl_in.at[key], zl_send, zl_recv, key, donor=donor - 1)
+
+    def finish(slot, carry):
+        turn = slot // donors
+        goal = target(lax.rem(slot, donors))
+        key = turn * donors + goal
+        swap(slot, row).wait_recv()
+        terms = [own_rows(slot, row), c_in.at[slot * chips + row]]
+        for step in range(1, chips):
+            hop = (step - 1) * 2 * donors + slot
             cross(hop, mine).wait_recv()
             terms.append(y_in.at[hop])
 
         @pl.when((goal >= donor) & (donor > 0))
         def _():
-            shift_right(goal).wait_recv()
+            shift_right(key).wait_recv()
 
         @pl.when((goal <= donor) & (donor < last))
         def _():
-            shift_left(goal).wait_recv()
+            shift_left(key).wait_recv()
 
         @pl.when(goal > donor)
         def _():
             @pl.when(donor == 0)
             def _():
-                add(zr_out.at[goal], *terms)
+                add(zr_out.at[key], *terms)
 
             @pl.when(donor > 0)
             def _():
-                add(zr_out.at[goal], zr_in.at[goal], *terms)
-
-            shift_right(goal).start()
+                add(zr_out.at[key], zr_in.at[key], *terms)
+
+            shift_right(key).start()
 
         @pl.when(goal < donor)
         def _():
             @pl.when(donor == last)
             def _():
-                add(zl_out.at[goal], *terms)
+                add(zl_out.at[key], *terms)
 
             @pl.when(donor < last)
             def _():
-                add(zl_out.at[goal], zl_in.at[goal], *terms)
-
-            shift_left(goal).start()
+                add(zl_out.at[key], zl_in.at[key], *terms)
+
+            shift_left(key).start()
 
         @pl.when(goal == donor)
         def _():
@@ -951,31 +972,34 @@
 
                     def body(index, carry):
                         at = pl.ds(pl.multiple_of(index * strip, strip), strip)
-                        down = pl.ds(pl.multiple_of(mine * suffix + index * strip, strip), strip)
+                        to = pl.ds(pl.multiple_of(turn * half + index * strip, strip), strip)
+                        down = pl.ds(
+                            pl.multiple_of(mine * suffix + turn * half + index * strip, strip), strip
+                        )
                         value = full_ref[donor * (columns // width) + part, down, :].astype(jnp.float32)
                         total = terms[0][at, wide].astype(jnp.float32)
                         for term in terms[1:] + ends:
                             total = total + term[at, wide].astype(jnp.float32)
-                        out_ref[at, wide] = (value + total).astype(out_ref.dtype)
+                        out_ref[to, wide] = (value + total).astype(out_ref.dtype)
                         return carry
 
-                    lax.fori_loop(0, suffix // strip, body, 0)
+                    lax.fori_loop(0, half // strip, body, 0)
 
             @pl.when(donor == 0)
             def _():
-                close([zl_in.at[donor]])
+                close([zl_in.at[key]])
 
             @pl.when(donor == last)
             def _():
-                close([zr_in.at[donor]])
+                close([zr_in.at[key]])
 
             @pl.when((donor > 0) & (donor < last))
             def _():
-                close([zl_in.at[donor], zr_in.at[donor]])
+                close([zl_in.at[key], zr_in.at[key]])
 
         return carry
 
-    lax.fori_loop(0, donors, finish, 0)
+    lax.fori_loop(0, 2 * donors, finish, 0)
 
     for step in range(1, blocks):
         gates_to(step).wait_send()
@@ -1007,23 +1031,24 @@
 
     lax.fori_loop(0, count, drain, 0)
 
-    def drain_blocks(goal, carry):
+    def drain_blocks(slot, carry):
+        goal = lax.rem(slot, donors)
         for step in range(chips):
-            swap(step * donors + goal).wait_send()
+            swap(slot, step).wait_send()
         for step in range(1, chips):
-            cross((step - 1) * donors + goal, mine).wait_send()
+            cross((step - 1) * 2 * donors + slot, mine).wait_send()
 
         @pl.when(goal > donor)
         def _():
-            shift_right(goal).wait_send()
+            shift_right(slot).wait_send()
 
         @pl.when(goal < donor)
         def _():
-            shift_left(goal).wait_send()
+            shift_left(slot).wait_send()
 
         return carry
 
-    lax.fori_loop(0, donors, drain_blocks, 0)
+    lax.fori_loop(0, 2 * donors, drain_blocks, 0)
 
 
 def page_kernel(
@@ -1167,7 +1192,7 @@
     kind = heads.dtype
     vmem = lambda *shape: pltpu.VMEM(shape, kind)
     wide = lambda *shape: pltpu.VMEM(shape, jnp.float32)
-    held = lambda number: pltpu.VMEM((number, suffix, columns), kind)
+    held = lambda number: pltpu.VMEM((2 * number, suffix // 2, columns), kind)
     return [
         vmem(blocks // donors, suffix, width),
         wide(blocks, 8, suffix),
@@ -1184,12 +1209,12 @@
         vmem(count, piece, width),
         vmem(blocks, tokens, width),
         vmem(model_width, 2 * ff_local),
-        vmem(2 * suffix, width),
+        vmem(tokens // 2, width),
         wide(tokens, 2 * ff_local),
         wide(tokens, 128),
         vmem(tokens, ff_local),
-        wide(2 * suffix, 1),
-        vmem(chips * donors, 2 * suffix, columns),
+        wide(tokens, 1),
+        vmem(2 * donors, tokens // 2, columns),
         held(chips * donors),
         held((chips - 1) * donors),
         held((chips - 1) * donors),
@@ -1225,10 +1250,10 @@
         + pair(count)
         + pair((chips - 1) * count)
         + pair(chips * count)
-        + pair(chips * donors)
-        + pair((chips - 1) * donors)
-        + pair(donors)
-        + pair(donors),
+        + pair(2 * chips * donors)
+        + pair(2 * (chips - 1) * donors)
+        + pair(2 * donors)
+        + pair(2 * donors),
         compiler_params=pltpu.CompilerParams(
             collective_id=3, has_side_effects=True, vmem_limit_bytes=VMEM_BYTES
         ),

time: 107 us -> 116 us (1.084)
  Pallas kernels: 102 us -> 111 us
    pallas_call x1, Pallas kernels: 85.8 us -> 95.1 us  [mix_blocks(): pl.pallas_call(functools.partial(mix_kernel, chips, donors, piece), out_s...]
where the time goes in v4:
time: 116 us
  Pallas kernels  111 us (96%)
  local copies, waits for them, and re-layouts  4.04 us (3%)
    pallas_call x1, Pallas kernels, mix_blocks(): pl.pallas_call(functools.partial(mix_kernel, chips, donors, piece), out_s...  95.1 us
    pallas_call x1, Pallas kernels, page_heads(): pl.pallas_call(functools.partial(page_kernel, experts, donors), out_shape...  16.4 us
    unnamed x7, local copies, waits for them, and re-layouts  3.9 us

profile of v4, /device:TPU:0, one launch (start us, length us, event | category | flops | bytes accessed | tf_op | source)
XLA Modules:
  0.0 116.2 jit_solution(15104283403941700795)
XLA Ops:
  0.6 0.0 copy-start
  0.7 0.9 copy-done
  1.5 0.1 constant_dynamic-slice_fusion
  1.7 0.6 copy.17
  2.3 16.4 %page_heads.1.heads_in = bf16[128,1024]{1,0:T(8,128)(2,1)} custom-call(bf16[4,2,32,256]{3,2,1,0:T(8,128)(2,1)} %pool_ref.1, s32[4,16]{1,0:T(4,128)} %table_ref.1, s32[4]{0:T(128)} %length_ref.1, bf16[128,1024]{1,0:T(8,128)(2,1)} %query_ref.1, bf16[128,256]{1,0:T(8,128)(2,1)} %bitcast.6), custom_call_target="tpu_custom_call" | custom-call | tf_op jit(solution)/shard_map/page_heads/pallas_call | solution.py:1168
  18.7 0.0 copy-start.1
  18.7 95.1 %mix_blocks.1 = bf16[128,1024]{1,0:T(8,128)(2,1)} custom-call(bf16[128,1024]{1,0:T(8,128)(2,1)} %page_heads.1.heads_in, bf16[32,128]{1,0:T(8,128)(2,1)} %bitcast.7, f32[4,128]{1,0:T(4,128)} %bitcast.8, s32[4,128]{1,0:T(4,128)} %bitcast.9, bf16[128,4096]{1,0:T(8,128)(2,1)} %hidden_hbm.1, bf16[1024,1024]{1,0:T(8,128)(2,1)} %outw_hbm.1, ...), custom_call_target="tpu_custom_call" | custom-call | tf_op jit(solution)/shard_map/mix_blocks/pallas_call | solution.py:1238
  113.8 1.7 %copy.20 = bf16[128,1024]{1,0:T(8,128)(2,1)} copy(bf16[128,1024]{1,0:T(8,128)(2,1)} %mix_blocks.1) | data formatting | bytes 524288
  115.5 0.0 copy-done.1
  115.5 0.7 copy.21
Async XLA Ops:
  0.6 0.9 copy-start
  18.7 96.8 %copy-start.1 = (bf16[128,1024]{1,0:T(8,128)(2,1)S(1)}, bf16[128,1024]{1,0:T(8,128)(2,1)}, u32[]{:S(2)}) copy-start(bf16[128,1024]{1,0:T(8,128)(2,1)} %page_heads.1.heads_in) | copy-start | bytes 786436

commit v5 on v3

--- a/solution.py
+++ b/solution.py
@@ -1156,6 +1156,11 @@
     )(pool, table, lengths, queries, fresh)
 
 
+def relay_steps(suffix, chips, donors, piece):
+    before_mix = 2 * suffix // piece + LAG + HOP * (donors // 2)
+    return min(16, 1 << (before_mix.bit_length() - 1))
+
+
 def mix_scratch(heads, out_weight, w_gate_up, chips, donors, piece):
     suffix, head_cols = heads.shape
     blocks = 2 * chips
@@ -1174,7 +1179,7 @@
         wide(blocks, 8, suffix),
         wide(model_width // 128, 128),
         vmem(head_cols, width),
-        vmem(3, model_width // 8, 2, ff_local),
+        vmem(3, model_width // relay_steps(suffix, chips, donors, piece), 2, ff_local),
         vmem(ff_local, model_width),
         vmem(tokens, head_cols),
         wide(tokens, width),
@@ -1216,7 +1221,7 @@
         in_specs=[inside] * 4 + [outside] * 4,
         out_specs=inside,
         scratch_shapes=scratch
-        + [dma((3,)), dma((8,))]
+        + [dma((3,)), dma((relay_steps(suffix, chips, donors, piece),))]
         + pair(2 * chips - 1)
         + pair(2 * chips // donors)
         + pair(chips - 1)

time: 107 us -> 105 us (0.981)
  Pallas kernels: 102 us -> 100 us
    pallas_call x1, Pallas kernels: 85.8 us -> 84.1 us  [mix_blocks(): pl.pallas_call(functools.partial(mix_kernel, chips, donors, piece), out_s...]
where the time goes in v5:
time: 105 us
  Pallas kernels  100 us (95%)
  local copies, waits for them, and re-layouts  4.04 us (4%)
    pallas_call x1, Pallas kernels, mix_blocks(): pl.pallas_call(functools.partial(mix_kernel, chips, donors, piece), out_s...  84.1 us
    pallas_call x1, Pallas kernels, page_heads(): pl.pallas_call(functools.partial(page_kernel, experts, donors), out_shape...  16.4 us
    unnamed x7, local copies, waits for them, and re-layouts  3.9 us

profile of v5, /device:TPU:0, one launch (start us, length us, event | category | flops | bytes accessed | tf_op | source)
XLA Modules:
  0.0 105.2 jit_solution(2715348546035743882)
XLA Ops:
  0.6 0.0 copy-start
  0.7 0.9 copy-done
  1.5 0.1 constant_dynamic-slice_fusion
  1.7 0.6 copy.17
  2.3 16.4 %page_heads.1.heads_in = bf16[128,1024]{1,0:T(8,128)(2,1)} custom-call(bf16[4,2,32,256]{3,2,1,0:T(8,128)(2,1)} %pool_ref.1, s32[4,16]{1,0:T(4,128)} %table_ref.1, s32[4]{0:T(128)} %length_ref.1, bf16[128,1024]{1,0:T(8,128)(2,1)} %query_ref.1, bf16[128,256]{1,0:T(8,128)(2,1)} %bitcast.6), custom_call_target="tpu_custom_call" | custom-call | tf_op jit(solution)/shard_map/page_heads/pallas_call | solution.py:1143
  18.7 0.0 copy-start.1
  18.7 84.1 %mix_blocks.1 = bf16[128,1024]{1,0:T(8,128)(2,1)} custom-call(bf16[128,1024]{1,0:T(8,128)(2,1)} %page_heads.1.heads_in, bf16[32,128]{1,0:T(8,128)(2,1)} %bitcast.7, f32[4,128]{1,0:T(4,128)} %bitcast.8, s32[4,128]{1,0:T(4,128)} %bitcast.9, bf16[128,4096]{1,0:T(8,128)(2,1)} %hidden_hbm.1, bf16[1024,1024]{1,0:T(8,128)(2,1)} %outw_hbm.1, ...), custom_call_target="tpu_custom_call" | custom-call | tf_op jit(solution)/shard_map/mix_blocks/pallas_call | solution.py:1218
  102.8 1.7 %copy.20 = bf16[128,1024]{1,0:T(8,128)(2,1)} copy(bf16[128,1024]{1,0:T(8,128)(2,1)} %mix_blocks.1) | data formatting | bytes 524288
  104.5 0.0 copy-done.1
  104.5 0.7 copy.21
Async XLA Ops:
  0.6 0.9 copy-start
  18.7 85.8 %copy-start.1 = (bf16[128,1024]{1,0:T(8,128)(2,1)S(1)}, bf16[128,1024]{1,0:T(8,128)(2,1)}, u32[]{:S(2)}) copy-start(bf16[128,1024]{1,0:T(8,128)(2,1)} %page_heads.1.heads_in) | copy-start | bytes 786436

commit v6 on v5

--- a/solution.py
+++ b/solution.py
@@ -1033,8 +1033,9 @@
     table_ref,
     length_ref,
     query_ref,
+    suffix_ref,
+    head_ref,
     fresh_ref,
-    head_ref,
     out_buf,
     pages_in,
     sends,
@@ -1094,6 +1095,12 @@
     for step_e, step_z in order:
         page(step_e, step_z).start()
     pages_in[mine] = out_buf[expert, donor * kv_heads // donors]
+    for group in range(kv_heads):
+
+        @pl.when(donor * kv_heads // donors == group)
+        def _():
+            fresh_ref[...] = suffix_ref[:, group, :]
+
     for step_e, step_z in order:
         from_e, from_z = ahead(experts - step_e, donors - step_z)
         send(
@@ -1136,7 +1143,7 @@
         page(step_e, step_z).wait_send()
 
 
-def page_heads(pool, table, lengths, queries, fresh, experts, donors):
+def page_heads(pool, table, lengths, queries, suffix_kv, experts, donors):
     seqs, kv_heads, page_len, both = pool.shape
     dma = pltpu.SemaphoreType.DMA
     inside = pl.BlockSpec(memory_space=pltpu.VMEM)
@@ -1146,6 +1153,7 @@
         in_specs=[inside] + [pl.BlockSpec(memory_space=pltpu.SMEM)] * 2 + [inside] * 2,
         out_specs=inside,
         scratch_shapes=[
+            pltpu.VMEM((queries.shape[0], both), pool.dtype),
             pltpu.VMEM((seqs, kv_heads, page_len, both), pool.dtype),
             pltpu.VMEM((experts * donors, page_len, both), pool.dtype),
             dma((experts * donors,)),
@@ -1153,7 +1161,7 @@
         ],
         compiler_params=pltpu.CompilerParams(collective_id=4, has_side_effects=True),
         name="page_heads",
-    )(pool, table, lengths, queries, fresh)
+    )(pool, table, lengths, queries, suffix_kv)
 
 
 def relay_steps(suffix, chips, donors, piece):
@@ -1274,12 +1282,11 @@
     owner_of = page_table // seq_count
     held_slot = jnp.sum(jnp.where(owner_of == owner_index, page_table % seq_count, 0), axis=1)
     chips = n_expert // 2
-    my_pair = lax.dynamic_index_in_dim(suffix_kv, my_group, 1, keepdims=False)
     scratch = mix_scratch(queries, out_weight, w_gate_up, chips, n_donor, PIECE)
     held_bytes = sum(math.prod(item.shape) * item.dtype.itemsize for item in scratch)
     if held_bytes <= VMEM_BYTES - 4 * 1024 * 1024:
         head_out = page_heads(
-            kv_pool, page_table, prefix_len, queries, my_pair, n_expert, n_donor
+            kv_pool, page_table, prefix_len, queries, suffix_kv, n_expert, n_donor
         )
         layer_out = mix_blocks(
             head_out,

time: 105 us -> 104 us (level)
  local copies, waits for them, and re-layouts: 4.04 us -> 2.38 us
    unnamed x7 -> x4, local copies, waits for them, and re-layouts: 3.9 us -> 2.38 us
where the time goes in v6:
time: 104 us
  Pallas kernels  101 us (97%)
  local copies, waits for them, and re-layouts  2.38 us (2%)
    pallas_call x1, Pallas kernels, mix_blocks(): pl.pallas_call(functools.partial(mix_kernel, chips, donors, piece), out_s...  84.1 us
    pallas_call x1, Pallas kernels, page_heads(): pl.pallas_call(functools.partial(page_kernel, experts, donors), out_shape...  16.5 us
    unnamed x4, local copies, waits for them, and re-layouts  2.38 us

profile of v6, /device:TPU:0, one launch (start us, length us, event | category | flops | bytes accessed | tf_op | source)
XLA Modules:
  0.0 103.6 jit_solution(9403640780945698492)
XLA Ops:
  0.6 16.5 %page_heads.1.heads_in = bf16[128,1024]{1,0:T(8,128)(2,1)} custom-call(bf16[4,2,32,256]{3,2,1,0:T(8,128)(2,1)} %pool_ref.1, s32[4,16]{1,0:T(4,128)} %table_ref.1, s32[4]{0:T(128)} %length_ref.1, bf16[128,1024]{1,0:T(8,128)(2,1)} %query_ref.1, bf16[128,2,256]{2,1,0:T(2,128)(2,1)} %suffix_ref.1), custom_call_target="tpu_custom_call" | custom-call | tf_op jit(solution)/shard_map/page_heads/pallas_call | solution.py:1150
  17.1 0.0 copy-start
  17.1 84.1 %mix_blocks.1 = bf16[128,1024]{1,0:T(8,128)(2,1)} custom-call(bf16[128,1024]{1,0:T(8,128)(2,1)} %page_heads.1.heads_in, bf16[32,128]{1,0:T(8,128)(2,1)} %bitcast.3, f32[4,128]{1,0:T(4,128)} %bitcast.4, s32[4,128]{1,0:T(4,128)} %bitcast.5, bf16[128,4096]{1,0:T(8,128)(2,1)} %hidden_hbm.1, bf16[1024,1024]{1,0:T(8,128)(2,1)} %outw_hbm.1, ...), custom_call_target="tpu_custom_call" | custom-call | tf_op jit(solution)/shard_map/mix_blocks/pallas_call | solution.py:1226
  101.2 1.7 %copy.16 = bf16[128,1024]{1,0:T(8,128)(2,1)} copy(bf16[128,1024]{1,0:T(8,128)(2,1)} %mix_blocks.1) | data formatting | bytes 524288
  102.9 0.0 copy-done
  102.9 0.7 copy.17
Async XLA Ops:
  17.1 85.8 %copy-start = (bf16[128,1024]{1,0:T(8,128)(2,1)S(1)}, bf16[128,1024]{1,0:T(8,128)(2,1)}, u32[]{:S(2)}) copy-start(bf16[128,1024]{1,0:T(8,128)(2,1)} %page_heads.1.heads_in) | copy-start | bytes 786436
